TPU v7x, 512 devices: a whole 4x4x16 slice. The times are simulated.
512 devices in a mesh: gx: 64 (over x, z), gy: 8 (over y, core).
Axes of the slice: x: 4, y: 4, z: 16, core: 2. Of those that a mesh axis runs over, the one named last changes fastest.
Arguments:
- members: bfloat16 [128, 64, 128, 256], P('gx', 'gy'), may hold values from -6 to 6
- obs_pert: bfloat16 [8, 131072, 256], P('gy', 'gx'), may hold values from -6 to 6
- obs_weight: bfloat16 [8, 131072], P('gy', 'gx'), may hold values from 0.019897461 to 0.5
- obs_innov: bfloat16 [8, 131072], P('gy', 'gx'), may hold values from -12 to 12
- obs_node: int32 [8, 131072, 1], P('gy', 'gx'), may hold values from 0 to 63; in each aligned block of 2048 rows (0 to 2047, 2048 to 4095, ..., all dimensions but the last counted through in order) at most 48 rows name the same one
- neighbour_slot: int32 [4, 128, 64], P(None, 'gx', 'gy'), may hold values from 0 to 8
- interp_weight: float32 [4, 128, 64], P(None, 'gx', 'gy'), may hold values from 0.1 to 1
Outputs:
- analysis: bfloat16 [128, 64, 128, 256], P('gx', 'gy')
Inputs may be any that keep to these rules, and one draw needn't show every extreme that they name: `obs_node`: within each device's aligned block of 2048 observations no node is named more than 48 times.
All inputs are finite; a program needn't handle non-finite values.
Results may differ from a plain program's by a relative error of at most 0.0063.
Values may be sent and summed in bfloat16 or wider, within the bound.
No kernel may reach another device: no remote copies, remote signals or barrier semaphores. Data moves between devices by JAX's collectives and lax.ppermute only.
A program may use at most 64 MiB of HBM per device.

v0:
```python
import jax
import jax.numpy as jnp
from jax import lax
from jax.sharding import PartitionSpec as P

NEWTON_STEPS = 8


inflation = 1.1


def with_halo(block, sides, width):
    for axis, dim in sides:
        count = lax.axis_size(axis)
        forward = [(i, i + 1) for i in range(count - 1)]
        forward.append((count - 1, 0))
        backward = [(target, source) for source, target in forward]
        low = lax.ppermute(
            lax.slice_in_dim(block, block.shape[dim] - width, None, axis=dim), axis, forward
        )
        high = lax.ppermute(lax.slice_in_dim(block, 0, width, axis=dim), axis, backward)
        block = jnp.concatenate([low, block, high], axis=dim)
    return block


def node_transform(pert, weight, innov):
    width = pert.shape[1]
    scaled = (pert.astype(jnp.float32) * weight.astype(jnp.float32)[:, None]).astype(jnp.bfloat16)
    gram = lax.dot_general(
        scaled, pert, (((0,), (0,)), ((), ())), preferred_element_type=jnp.float32
    )
    identity = jnp.eye(width, dtype=jnp.float32)
    gram = gram + (width - 1) / inflation * identity
    rhs = jnp.dot(innov[None, :], scaled, preferred_element_type=jnp.float32)[0]
    total = jnp.trace(gram)
    current_iterate = gram / total
    root = identity
    for step in range(NEWTON_STEPS):
        middle = 1.5 * identity - 0.5 * jnp.dot(
            root, current_iterate, precision=lax.Precision.HIGHEST
        )
        current_iterate = jnp.dot(current_iterate, middle, precision=lax.Precision.HIGHEST)
        root = jnp.dot(middle, root, precision=lax.Precision.HIGHEST)
    inverse = jnp.dot(root, root, precision=lax.Precision.HIGHEST) / total
    mean_weight = jnp.dot(inverse, rhs, precision=lax.Precision.HIGHEST)
    transform = mean_weight[:, None] + jnp.sqrt((width - 1) / total) * root
    return transform.astype(jnp.bfloat16)


def shards(members, obs_pert, obs_weight, obs_innov, obs_node, neighbour_slot, interp_weight):
    pert = obs_pert[0]
    weight = obs_weight[0]
    innov = obs_innov[0]
    nodes = obs_node[0, :, 0]
    targets = lax.axis_size("gx")
    width = pert.shape[1]
    capacity = 3 * pert.shape[0] // (2 * targets)
    onehot = (nodes[:, None] == jnp.arange(targets, dtype=jnp.int32)[None, :]).astype(jnp.int32)
    rank = jnp.sum(jnp.cumsum(onehot, 0) * onehot, 1) - 1
    slot = nodes * capacity + rank
    count = targets * capacity
    sent_pert = (
        jnp.zeros((count, width), jnp.bfloat16).at[slot].set(pert).reshape(targets, capacity, width)
    )
    sent_weight = jnp.zeros((count,), jnp.bfloat16).at[slot].set(weight).reshape(targets, capacity)
    sent_innov = jnp.zeros((count,), jnp.bfloat16).at[slot].set(innov).reshape(targets, capacity)
    got_pert, got_weight, got_innov = (
        lax.all_to_all(sent_pert, "gx", split_axis=0, concat_axis=0, tiled=True),
        lax.all_to_all(sent_weight, "gx", split_axis=0, concat_axis=0, tiled=True),
        lax.all_to_all(sent_innov, "gx", split_axis=0, concat_axis=0, tiled=True),
    )
    transform = node_transform(
        got_pert.reshape(count, width), got_weight.reshape(count), got_innov.reshape(count)
    )
    local = transform[None, None]
    stencil = with_halo(local, (("gx", 0), ("gy", 1)), 1)
    table = stencil.reshape(9, width, width).astype(jnp.float32)
    columns = members.shape[0] * members.shape[1]
    levels = members.shape[2]
    slots = neighbour_slot.reshape(4, columns)
    share = interp_weight.reshape(4, columns)
    share = share / jnp.sum(share, 0)
    matches = (slots[:, :, None] == jnp.arange(9, dtype=jnp.int32)[None, None, :]).astype(
        jnp.float32
    )
    coefficient = jnp.sum(share[:, :, None] * matches, 0)
    blend_factor = jnp.tensordot(
        coefficient, table, axes=1, precision=lax.Precision.HIGHEST
    ).astype(jnp.bfloat16)
    state = members.reshape(columns, levels, width)
    mean = jnp.mean(state.astype(jnp.float32), -1)
    member_anomaly = (state.astype(jnp.float32) - mean[..., None]).astype(jnp.bfloat16)
    update_matrix = jnp.einsum(
        "frt,fty->fry", member_anomaly, blend_factor, preferred_element_type=jnp.float32
    )
    result = (mean[..., None] + update_matrix).astype(jnp.bfloat16)
    return result.reshape(members.shape)


def solution(mesh):
    return jax.shard_map(
        shards,
        mesh=mesh,
        in_specs=(
            P("gx", "gy", None, None),
            P("gy", "gx", None),
            P("gy", "gx"),
            P("gy", "gx"),
            P("gy", "gx", None),
            P(None, "gx", "gy"),
            P(None, "gx", "gy"),
        ),
        out_specs=P("gx", "gy", None, None),
        check_vma=False,
    )
```

profile of v0, /device:TPU:25, one launch (start us, length us, event | category | flops | bytes accessed | tf_op | source)
XLA Modules:
  0.0 226.5 jit_solution(5890879359784634576)
XLA Ops:
  0.0 0.8 fusion.24
  0.8 18.1 %reduce-window.6 = s32[64,16,128]{2,1,0:T(8,128)S(1)} reduce-window(s32[64,16,128]{2,1,0:T(8,128)S(1)} %fusion.24, s32[]{:T(128)} %constant.16.clone.1), window={size=1x1x128 pad=0_0x0_0x127_0}, to_apply=%region_3.4 | reduce-window | flops 16646144 | bytes 1048580 | tf_op jit(solution)/shard_map/reduce-window
  19.0 0.2 slice.8
  19.2 0.4 copy.30
  19.6 0.2 reduce-window.9
  19.8 0.2 broadcast_add_fusion
  20.0 0.2 fusion.23
  20.3 14.6 %scatter_custom_fusion.1 = bf16[3072]{0:T(1024)(128)(2,1)S(1)} fusion(s32[2048]{0:T(1024)S(1)} %bitcast.112, bf16[2048]{0:T(1024)(128)(2,1)S(1)} %reduce.2, bf16[]{:T(256)} %constant.10.clone.1), kind=kCustom, calls=%fused_computation.61 | custom fusion | bytes 6146 | tf_op jit(solution)/shard_map/scatter | solution.py:65
  34.9 0.7 all_to_all.20
  35.6 18.3 %all-to-all-start.1 = ((bf16[64,1,48]{2,1,0:T(2,128)(2,1)}), bf16[64,1,48]{2,1,0:T(2,128)(2,1)S(1)}, u32[]{:S(2)}, u32[]{:S(2)}) async-start(bf16[64,1,48]{2,1,0:T(2,128)(2,1)} %all_to_all.20), calls=%async_computation.1 | async-start | bytes 65536 | tf_op jit(solution)/shard_map/all_to_all | solution.py:69
  53.9 14.6 %scatter_custom_fusion.2 = bf16[3072]{0:T(1024)(128)(2,1)S(1)} fusion(s32[2048]{0:T(1024)S(1)} %bitcast.113, bf16[2048]{0:T(1024)(128)(2,1)S(1)} %reduce.3, bf16[]{:T(256)} %constant.10.clone.1), kind=kCustom, calls=%fused_computation.59 | custom fusion | bytes 6146 | tf_op jit(solution)/shard_map/scatter | solution.py:66
  68.5 0.7 all_to_all.21
  69.2 14.7 %all-to-all-start.2 = ((bf16[64,1,48]{2,1,0:T(2,128)(2,1)}), bf16[64,1,48]{2,1,0:T(2,128)(2,1)S(1)}, u32[]{:S(2)}, u32[]{:S(2)}) async-start(bf16[64,1,48]{2,1,0:T(2,128)(2,1)} %all_to_all.21), calls=%async_computation.2 | async-start | bytes 65536 | tf_op jit(solution)/shard_map/all_to_all | solution.py:70
  84.0 10.6 %scatter_custom_fusion = bf16[3072,256]{1,0:T(8,128)(2,1)} fusion(s32[2048]{0:T(1024)S(1)} %bitcast.114, bf16[1,2048,256]{2,1,0:T(8,128)(2,1)S(1)} %copy-done, bf16[]{:T(256)} %constant.10.clone.1), kind=kCustom, calls=%fused_computation.33 | custom fusion | bytes 2621442 | tf_op jit(solution)/shard_map/scatter | solution.py:63
  94.6 2.4 %all-to-all-done.2 = bf16[64,1,48]{2,1,0:T(2,128)(2,1)S(1)} async-done(((bf16[64,1,48]{2,1,0:T(2,128)(2,1)}), bf16[64,1,48]{2,1,0:T(2,128)(2,1)S(1)}, u32[]{:S(2)}, u32[]{:S(2)}) %all-to-all-start.2) | async-done | bytes 6176 | tf_op jit(solution)/shard_map/all_to_all | solution.py:70
  97.0 12.1 %all-to-all-start = ((bf16[64,48,256]{2,1,0:T(8,128)(2,1)}), bf16[64,48,256]{2,1,0:T(8,128)(2,1)S(1)}, u32[]{:S(2)}, u32[]{:S(2)}) async-start(bf16[64,48,256]{2,1,0:T(8,128)(2,1)} %bitcast.102), calls=%async_computation | async-start | bytes 3145728 | tf_op jit(solution)/shard_map/all_to_all | solution.py:68
  109.1 0.1 reshape.134
  109.2 0.1 div.38
  109.3 1.6 convert_reduce_fusion
  110.9 0.1 reduce.4
  111.0 0.1 reshape.167
  111.1 68.3 %all-to-all-done = bf16[64,48,256]{2,1,0:T(8,128)(2,1)S(1)} async-done(((bf16[64,48,256]{2,1,0:T(8,128)(2,1)}), bf16[64,48,256]{2,1,0:T(8,128)(2,1)S(1)}, u32[]{:S(2)}, u32[]{:S(2)}) %all-to-all-start) | async-done | bytes 1572896 | tf_op jit(solution)/shard_map/all_to_all | solution.py:68
  179.4 1.8 select_reduce_fusion
  181.2 1.0 fusion.17
  182.2 1.0 fusion.27
  183.2 0.3 fusion.25
  183.5 0.4 fusion.16
  183.9 0.4 fusion.34
  184.3 0.4 fusion.33
  184.7 0.4 fusion.15
  185.0 0.4 fusion.36
  185.4 0.4 fusion.35
  185.8 0.4 fusion.14
  186.2 0.4 fusion.38
  186.6 0.4 fusion.37
  187.0 0.4 fusion.13
  187.4 0.4 fusion.40
  187.8 0.4 fusion.39
  188.1 0.4 fusion.12
  188.5 0.4 fusion.42
  188.9 0.4 fusion.41
  189.3 0.4 fusion.11
  189.7 0.4 fusion.44
  190.1 0.4 fusion.43
  190.5 0.4 fusion.10
  190.9 0.4 fusion.45
  191.2 1.0 convolution_divide_fusion
  193.0 0.5 multiply_convert_fusion
  193.5 0.3 convolution_bitcast_fusion.1
  193.8 0.3 fusion.46
  194.1 0.2 fusion.26
  194.3 6.9 %collective-permute-start = (bf16[1,1,256,256]{3,2,1,0:T(8,128)(2,1)S(1)}, bf16[1,1,256,256]{3,2,1,0:T(8,128)(2,1)S(1)}, u32[]{:S(2)}, u32[]{:S(2)}) collective-permute-start(bf16[1,1,256,256]{3,2,1,0:T(8,128)(2,1)S(1)} %fusion.26), channel_id=1, source_target_pairs={{0,8},{8,16},{16,24},{24,32},{32,40},{40,48},{48,56},{56,64},{64,7... | collective-permute-start | bytes 393224 | tf_op jit(solution)/shard_map/ppermute | solution.py:18
  201.2 2.1 collective-permute-start.1
  203.3 3.5 %collective-permute-done.1 = bf16[1,1,256,256]{3,2,1,0:T(8,128)(2,1)S(1)} collective-permute-done((bf16[1,1,256,256]{3,2,1,0:T(8,128)(2,1)S(1)}, bf16[1,1,256,256]{3,2,1,0:T(8,128)(2,1)S(1)}, u32[]{:S(2)}, u32[]{:S(2)}) %collective-permute-start.1) | collective-permute-done | bytes 131104 | tf_op jit(solution)/shard_map/ppermute | solution.py:21
  206.9 0.8 pad_maximum_fusion.1
  207.7 5.8 %collective-permute-start.2 = (bf16[3,1,256,256]{3,2,1,0:T(8,128)(2,1)}, bf16[3,1,256,256]{3,2,1,0:T(8,128)(2,1)S(1)}, u32[]{:S(2)}, u32[]{:S(2)}) collective-permute-start(bf16[3,1,256,256]{3,2,1,0:T(8,128)(2,1)} %pad_maximum_fusion.1), channel_id=1, source_target_pairs={{0,1},{1,2},{2,3},{3,4},{4,5},{5,6},{6,7},{7,0},{8,9},{9,10},{10,1... | collective-permute-start | bytes 1179656 | tf_op jit(solution)/shard_map/ppermute | solution.py:18
  213.4 0.2 collective-permute-start.3
  213.6 0.1 eq.67
  213.7 0.3 fusion
  214.1 4.4 %collective-permute-done.2 = bf16[3,1,256,256]{3,2,1,0:T(8,128)(2,1)S(1)} collective-permute-done((bf16[3,1,256,256]{3,2,1,0:T(8,128)(2,1)}, bf16[3,1,256,256]{3,2,1,0:T(8,128)(2,1)S(1)}, u32[]{:S(2)}, u32[]{:S(2)}) %collective-permute-start.2) | collective-permute-done | bytes 393248 | tf_op jit(solution)/shard_map/ppermute | solution.py:18
  218.5 3.6 %collective-permute-done.3 = bf16[3,1,256,256]{3,2,1,0:T(8,128)(2,1)S(1)} collective-permute-done((bf16[3,1,256,256]{3,2,1,0:T(8,128)(2,1)}, bf16[3,1,256,256]{3,2,1,0:T(8,128)(2,1)S(1)}, u32[]{:S(2)}, u32[]{:S(2)}) %collective-permute-start.3) | collective-permute-done | bytes 393248 | tf_op jit(solution)/shard_map/ppermute | solution.py:21
  222.1 0.1 pad_maximum_fusion
  222.2 2.5 %fusion.5 = bf16[16,256,256]{2,0,1:T(8,128)(2,1)S(1)} fusion(bf16[9,256,256]{2,1,0:T(8,128)(2,1)S(1)} %bitcast.101, f32[16,9]{0,1:T(8,128)S(1)} %select_reduce_fusion.1), kind=kOutput, calls=%fused_computation.11 | convolution fusion | flops 114294784 | bytes 3277376 | tf_op jit(solution)/shard_map/dot_general | solution.py:87
  224.7 1.8 add_convert_fusion
  (25 shorter events, 0.2 us)
Async XLA Ops:
  0.0 84.0 %copy-start = (bf16[1,2048,256]{2,1,0:T(8,128)(2,1)S(1)}, bf16[1,2048,256]{2,1,0:T(8,128)(2,1)}, u32[]{:S(2)}) copy-start(bf16[1,2048,256]{2,1,0:T(8,128)(2,1)} %param.8) | copy-start | bytes 3145732
  19.0 1.1 copy-start.2
  19.0 1.3 copy-start.4
  19.0 34.9 %copy-start.5 = (bf16[1,2048]{1,0:T(2,128)(2,1)S(1)}, bf16[1,2048]{1,0:T(2,128)(2,1)}, u32[]{:S(2)}) copy-start(bf16[1,2048]{1,0:T(2,128)(2,1)} %param.10) | copy-start | bytes 12292
  35.6 33.6 %all-to-all-start.1 = ((bf16[64,1,48]{2,1,0:T(2,128)(2,1)}), bf16[64,1,48]{2,1,0:T(2,128)(2,1)S(1)}, u32[]{:S(2)}, u32[]{:S(2)}) async-start(bf16[64,1,48]{2,1,0:T(2,128)(2,1)} %all_to_all.20), calls=%async_computation.1 | async-start | bytes 65536 | tf_op jit(solution)/shard_map/all_to_all | solution.py:69
  69.2 27.7 %all-to-all-start.2 = ((bf16[64,1,48]{2,1,0:T(2,128)(2,1)}), bf16[64,1,48]{2,1,0:T(2,128)(2,1)S(1)}, u32[]{:S(2)}, u32[]{:S(2)}) async-start(bf16[64,1,48]{2,1,0:T(2,128)(2,1)} %all_to_all.21), calls=%async_computation.2 | async-start | bytes 65536 | tf_op jit(solution)/shard_map/all_to_all | solution.py:70
  97.0 12.1 %copy-start.3 = (f32[4,2,8]{2,1,0:T(2,128)S(1)}, f32[4,2,8]{2,1,0:T(2,128)}, u32[]{:S(2)}) copy-start(f32[4,2,8]{2,1,0:T(2,128)} %param.13) | copy-start | bytes 772
  97.0 82.5 %all-to-all-start = ((bf16[64,48,256]{2,1,0:T(8,128)(2,1)}), bf16[64,48,256]{2,1,0:T(8,128)(2,1)S(1)}, u32[]{:S(2)}, u32[]{:S(2)}) async-start(bf16[64,48,256]{2,1,0:T(8,128)(2,1)} %bitcast.102), calls=%async_computation | async-start | bytes 3145728 | tf_op jit(solution)/shard_map/all_to_all | solution.py:68
  193.5 20.1 %copy-start.6 = (s32[4,2,8]{2,1,0:T(2,128)S(1)}, s32[4,2,8]{2,1,0:T(2,128)}, u32[]{:S(2)}) copy-start(s32[4,2,8]{2,1,0:T(2,128)} %param.12) | copy-start | bytes 772
  193.5 20.2 %copy-start.1 = (bf16[2,8,128,256]{3,2,1,0:T(8,128)(2,1)S(1)}, bf16[2,8,128,256]{3,2,1,0:T(8,128)(2,1)}, u32[]{:S(2)}) copy-start(bf16[2,8,128,256]{3,2,1,0:T(8,128)(2,1)} %param.7) | copy-start | bytes 3145732
  194.3 9.1 %collective-permute-start = (bf16[1,1,256,256]{3,2,1,0:T(8,128)(2,1)S(1)}, bf16[1,1,256,256]{3,2,1,0:T(8,128)(2,1)S(1)}, u32[]{:S(2)}, u32[]{:S(2)}) collective-permute-start(bf16[1,1,256,256]{3,2,1,0:T(8,128)(2,1)S(1)} %fusion.26), channel_id=1, source_target_pairs={{0,8},{8,16},{16,24},{24,32},{32,40},{40,48},{48,56},{56,64},{64,7... | collective-permute-start | bytes 393224 | tf_op jit(solution)/shard_map/ppermute | solution.py:18
  201.2 5.7 %collective-permute-start.1 = (bf16[1,1,256,256]{3,2,1,0:T(8,128)(2,1)S(1)}, bf16[1,1,256,256]{3,2,1,0:T(8,128)(2,1)S(1)}, u32[]{:S(2)}, u32[]{:S(2)}) collective-permute-start(bf16[1,1,256,256]{3,2,1,0:T(8,128)(2,1)S(1)} %fusion.26), channel_id=1, source_target_pairs={{8,0},{16,8},{24,16},{32,24},{40,32},{48,40},{56,48},{64,56},{72,6... | collective-permute-start | bytes 393224 | tf_op jit(solution)/shard_map/ppermute | solution.py:21
  207.7 10.8 %collective-permute-start.2 = (bf16[3,1,256,256]{3,2,1,0:T(8,128)(2,1)}, bf16[3,1,256,256]{3,2,1,0:T(8,128)(2,1)S(1)}, u32[]{:S(2)}, u32[]{:S(2)}) collective-permute-start(bf16[3,1,256,256]{3,2,1,0:T(8,128)(2,1)} %pad_maximum_fusion.1), channel_id=1, source_target_pairs={{0,1},{1,2},{2,3},{3,4},{4,5},{5,6},{6,7},{7,0},{8,9},{9,10},{10,1... | collective-permute-start | bytes 1179656 | tf_op jit(solution)/shard_map/ppermute | solution.py:18
  213.4 8.6 %collective-permute-start.3 = (bf16[3,1,256,256]{3,2,1,0:T(8,128)(2,1)}, bf16[3,1,256,256]{3,2,1,0:T(8,128)(2,1)S(1)}, u32[]{:S(2)}, u32[]{:S(2)}) collective-permute-start(bf16[3,1,256,256]{3,2,1,0:T(8,128)(2,1)} %pad_maximum_fusion.1), channel_id=1, source_target_pairs={{1,0},{2,1},{3,2},{4,3},{5,4},{6,5},{7,6},{0,7},{9,8},{10,9},{11,1... | collective-permute-start | bytes 1179656 | tf_op jit(solution)/shard_map/ppermute | solution.py:21
where the time goes:
time: 228 us; the launch traced here: 227 us
  waiting for transfers between devices  82.2 us (36%)
  starting transfers between devices  60.1 us (26%)
  local copies, waits for them, and re-layouts  42.1 us (18%)
  other arithmetic  23.3 us (10%)
  matrix products  17.6 us (8%)
    all_to_all x1, waiting for transfers between devices, shards(): lax.all_to_all(sent_pert, 'gx', split_axis=0, concat_axis=0, tiled=True)  68.3 us
    another operation x3, other arithmetic  18.5 us
    all_to_all x1, starting transfers between devices, shards(): lax.all_to_all(sent_weight, 'gx', split_axis=0, concat_axis=0, tiled=True)  18.3 us
    all_to_all x1, starting transfers between devices, shards(): lax.all_to_all(sent_innov, 'gx', split_axis=0, concat_axis=0, tiled=True)  14.7 us
    scatter x1, local copies, waits for them, and re-layouts, shards(): jnp.zeros((count,), jnp.bfloat16).at[slot].set(innov)  14.6 us
    scatter x1, local copies, waits for them, and re-layouts, shards(): jnp.zeros((count,), jnp.bfloat16).at[slot].set(weight)  14.6 us
    ppermute x2, starting transfers between devices, with_halo(): lax.ppermute(lax.slice_in_dim(block, block.shape[dim] - width, None, axis...  12.7 us
    all_to_all x1, starting transfers between devices, shards(): lax.all_to_all(sent_pert, 'gx', split_axis=0, concat_axis=0, tiled=True)  12.1 us
  transfers between devices with their start and end apart: 7, of which 5 were waited for; matrix products, arithmetic and copies ran while one was open for 12% of the time, Pallas kernels for 0%

commit v1 on v0

v1 whole, which is shorter than its diff:
```python
import jax
import jax.numpy as jnp
from jax import lax
from jax.experimental import pallas as pl
from jax.experimental.pallas import tpu as pltpu
from jax.sharding import Mesh
from jax.sharding import PartitionSpec as P

NEWTON_STEPS = 8
inflation = 1.1

SHAPE = (4, 8, 2, 4, 2)
AXES = ("x", "zh", "zl", "y", "c")
GX = ("x", "zh", "zl")
GY = ("y", "c")

NODES = 64
HIGH = 8
GROUP = 8
CAP = 48
OBS = 2048
K = 256
HALF = 128
ROWS = HIGH * CAP + 16
PACKED = K + 8
WIRE = jnp.bfloat16
F32 = jnp.float32
BF16 = jnp.bfloat16


def iota(shape, dim):
    return lax.broadcasted_iota(jnp.int32, shape, dim)


def route_kernel(node_ref, weight_ref, innov_ref, pert_ref, out_ref, rank_ref, scaled_ref, rhs_ref):
    step = pl.program_id(0)

    @pl.when(step == 0)
    def _():
        row = iota((NODES, 1), 0)
        name = (row // 16) * 16 + (row % 8) * 2 + (row // 8) % 2
        onehot = (node_ref[...] == name).astype(F32)
        upper = (iota((K, K), 0) <= iota((K, K), 1)).astype(BF16)
        carry = jnp.zeros((NODES, 1), F32)
        for b in range(OBS // K):
            part = onehot[:, b * K : (b + 1) * K]
            count = jnp.dot(part.astype(BF16), upper, preferred_element_type=F32) + carry
            rank_ref[:, b * K : (b + 1) * K] = jnp.where(part > 0, count - 1.0, -1.0)
            carry = count[:, K - 1 : K]
        weight = weight_ref[...].astype(F32)
        side = jnp.sqrt(weight)
        side = jnp.concatenate([side[:, k * 128 : (k + 1) * 128] for k in range(OBS // 128)], 0).T
        for k in range(OBS // 128):
            rows = pl.ds(k * 128, 128)
            scaled_ref[rows, :] = (pert_ref[rows, :].astype(F32) * side[:, k : k + 1]).astype(BF16)
        factor = onehot * (weight * innov_ref[...].astype(F32))
        top = factor.astype(BF16)
        rest = (factor - top.astype(F32)).astype(BF16)
        both = jnp.dot(jnp.concatenate([top, rest], 0), pert_ref[...], preferred_element_type=F32)
        rhs_ref[...] = both[:NODES] + both[NODES:]

    rank = rank_ref[pl.ds(pl.multiple_of(step * HIGH, HIGH), HIGH), :]
    wanted = iota((CAP, OBS), 0).astype(F32)
    pick = jnp.concatenate([(rank[h : h + 1, :] == wanted).astype(BF16) for h in range(HIGH)], 0)
    out_ref[0, : HIGH * CAP, :] = jnp.dot(
        pick, scaled_ref[...], preferred_element_type=F32
    ).astype(BF16)
    rhs = rhs_ref[pl.ds(pl.multiple_of(step * HIGH, HIGH), HIGH), :]
    top = rhs.astype(BF16).astype(F32)
    out_ref[0, HIGH * CAP :, :] = jnp.concatenate([top, rhs - top], 0).astype(BF16)


def route(node, weight, innov, pert):
    whole = lambda shape: pl.BlockSpec(shape, lambda d: (0, 0))
    return pl.pallas_call(
        route_kernel,
        grid=(GROUP,),
        in_specs=[whole((1, OBS)), whole((1, OBS)), whole((1, OBS)), whole((OBS, K))],
        out_specs=pl.BlockSpec((1, ROWS, K), lambda d: (d, 0, 0)),
        out_shape=jax.ShapeDtypeStruct((GROUP, ROWS, K), BF16),
        scratch_shapes=[
            pltpu.VMEM((NODES, OBS), F32),
            pltpu.VMEM((OBS, K), BF16),
            pltpu.VMEM((NODES, K), F32),
        ],
        name="route",
    )(node, weight, innov, pert)


def gram_kernel(obs_ref, side_ref, out_ref):
    step = pl.program_id(0)
    obs = obs_ref[...].reshape(GROUP * CAP, K)
    gram = lax.dot_general(obs, obs, (((0,), (0,)), ((), ())), preferred_element_type=F32)
    first, cross, last = gram[:HALF, :HALF], gram[:HALF, HALF:], gram[HALF:, HALF:]
    low, high = iota((HALF, HALF), 0), iota((HALF, HALF), 1)
    eye = low == high
    first_diag = jnp.sum(jnp.where(eye, first, 0.0), 0, keepdims=True)
    last_diag = jnp.sum(jnp.where(eye, last, 0.0), 0, keepdims=True)
    sides = jnp.sum(side_ref[...].astype(F32), 0)
    mine = iota((16, K), 0) % HIGH == step
    rhs = jnp.sum(jnp.where(mine, sides, 0.0), 0, keepdims=True)
    out_ref[0, :HALF, :] = jnp.where(low <= high, first, last).astype(WIRE)
    out_ref[0, HALF:K, :] = cross.astype(WIRE)
    rest = lambda v: v - v.astype(WIRE).astype(F32)
    extra = jnp.concatenate(
        [
            last_diag,
            rest(last_diag),
            rest(first_diag),
            rhs[:, :HALF],
            rhs[:, HALF:],
            rest(rhs[:, :HALF]),
            rest(rhs[:, HALF:]),
            jnp.zeros((1, HALF), F32),
        ],
        0,
    )
    out_ref[0, K:, :] = extra.astype(WIRE)


def partial_grams(got):
    return pl.pallas_call(
        gram_kernel,
        grid=(HIGH,),
        in_specs=[
            pl.BlockSpec((GROUP, CAP, K), lambda h: (0, h, 0)),
            pl.BlockSpec((GROUP, 16, K), lambda h: (0, HIGH * CAP // 16, 0)),
        ],
        out_specs=pl.BlockSpec((1, PACKED, HALF), lambda h: (h, 0, 0)),
        out_shape=jax.ShapeDtypeStruct((HIGH, PACKED, HALF), WIRE),
        name="gram",
    )(got, got)


def split(a):
    top = a.astype(BF16)
    return top, (a - top.astype(F32)).astype(BF16)


def dot3(a, b):
    (a_top, a_rest), (b_top, b_rest) = a, b
    dot = lambda u, v: jnp.dot(u, v, preferred_element_type=F32)
    return dot(a_top, b_top) + (dot(a_top, b_rest) + dot(a_rest, b_top))


def newton_kernel(got_ref, out_ref):
    packed = jnp.sum(got_ref[...].astype(F32), 0)
    mixed, cross, extra = packed[:HALF], packed[HALF:K], packed[K:]
    low, high = iota((HALF, HALF), 0), iota((HALF, HALF), 1)
    eye = low == high
    base = (K - 1) / inflation
    upper = jnp.where(low < high, mixed, 0.0)
    lower = jnp.where(low > high, mixed, 0.0)
    first_diag = jnp.where(eye, mixed + extra[2:3] + base, 0.0)
    last_diag = jnp.where(eye, extra[0:1] + extra[1:2] + base, 0.0)
    first = upper + upper.T + first_diag
    last = lower + lower.T + last_diag
    gram = jnp.concatenate(
        [jnp.concatenate([first, cross], 1), jnp.concatenate([cross.T, last], 1)], 0
    )
    rhs = jnp.concatenate([extra[3:4] + extra[5:6], extra[4:5] + extra[6:7]], 1)
    total = jnp.sum(jnp.sum(first_diag + last_diag, 1, keepdims=True), 0, keepdims=True)
    identity = (iota((K, K), 0) == iota((K, K), 1)).astype(F32)
    error = gram / total
    root = None
    for step in range(NEWTON_STEPS):
        middle = 1.5 * identity - 0.5 * error
        middle_parts = split(middle)
        root = middle if step == 0 else dot3(split(root), middle_parts)
        if step < NEWTON_STEPS - 1:
            error = dot3(split(error), middle_parts)
            error = dot3(split(error), middle_parts)
    once = jnp.dot(
        jnp.broadcast_to(rhs, (8, K)), root, precision=lax.Precision.HIGHEST, preferred_element_type=F32
    )[:1]
    mean_weight = jnp.sum(root * once, 1, keepdims=True) / total
    out_ref[...] = (mean_weight + jnp.sqrt((K - 1) / total) * root).astype(BF16)


def node_transform(got):
    return pl.pallas_call(
        newton_kernel,
        out_shape=jax.ShapeDtypeStruct((K, K), BF16),
        name="newton",
    )(got)


def analysis_kernel(slot_ref, share_ref, table_ref, state_ref, out_ref):
    step = pl.program_id(0)
    for n in range(COLS):
        column = step * COLS + n
        blend = share_ref[0, column] * table_ref[slot_ref[0, column]].astype(F32)
        for q in range(1, 4):
            blend += share_ref[q, column] * table_ref[slot_ref[q, column]].astype(F32)
        state = state_ref[n].astype(F32)
        mean = jnp.mean(state, -1, keepdims=True)
        anomaly = (state - mean).astype(BF16)
        update = jnp.dot(anomaly, blend.astype(BF16), preferred_element_type=F32)
        out_ref[n] = (mean + update).astype(BF16)


COLS = 4


def analyse(slots, share, table, state):
    columns, levels, width = state.shape
    block = pl.BlockSpec((COLS, levels, width), lambda f, *_: (f, 0, 0))
    return pl.pallas_call(
        analysis_kernel,
        grid_spec=pltpu.PrefetchScalarGridSpec(
            num_scalar_prefetch=2,
            grid=(columns // COLS,),
            in_specs=[pl.BlockSpec((9, K, K), lambda f, *_: (0, 0, 0)), block],
            out_specs=block,
        ),
        out_shape=jax.ShapeDtypeStruct(state.shape, BF16),
        name="analysis",
    )(slots, share, table, state)


def swap(block, axes, count):
    even = [(i, i ^ 1) for i in range(count)]
    odd = [(i, (((i + 1) ^ 1) - 1) % count) for i in range(count)]
    return lax.ppermute(block, axes, even), lax.ppermute(block, axes, odd)


def shards(members, obs_pert, obs_weight, obs_innov, obs_node, neighbour_slot, interp_weight):
    sent = route(obs_node.reshape(1, OBS), obs_weight, obs_innov, obs_pert[0])
    got = lax.all_to_all(sent, ("x", "zl"), split_axis=0, concat_axis=0, tiled=True)
    grams = partial_grams(got)
    grams = lax.all_to_all(grams, "zh", split_axis=0, concat_axis=0, tiled=True)
    own = node_transform(grams)
    even, odd = swap(own, GX, 64)
    line = jnp.stack([even, own, odd])
    even, odd = swap(line, GY, 8)
    table = jnp.concatenate([even, line, odd])
    columns = members.shape[0] * members.shape[1]
    slots = neighbour_slot.reshape(4, columns)
    share = interp_weight.reshape(4, columns)
    share = share / jnp.sum(share, 0)

    def place(offset, axes):
        flip = lax.axis_index(axes) % 2 == 1
        return jnp.where(flip, offset, 2 - offset)

    slots = place(slots % 3, GY) * 3 + place(slots // 3, GX)
    state = members.reshape(columns, *members.shape[2:])
    return analyse(slots, share, table, state).reshape(members.shape)


def solution(mesh):
    fine = Mesh(mesh.devices.reshape(SHAPE), AXES)
    return jax.shard_map(
        shards,
        mesh=fine,
        in_specs=(
            P(GX, GY, None, None),
            P(GY, GX, None),
            P(GY, GX),
            P(GY, GX),
            P(GY, GX, None),
            P(None, GX, GY),
            P(None, GX, GY),
        ),
        out_specs=P(GX, GY, None, None),
        check_vma=False,
    )
```

time: 228 us -> 129 us (0.57)
  waiting for transfers between devices: 82.2 us -> 40.9 us
  local copies, waits for them, and re-layouts: 42.1 us -> 2.33 us
  starting transfers between devices: 60.1 us -> 29.4 us
  blocking collectives: 0 us -> 26.9 us
  Pallas kernels: 0 us -> 26.6 us
  other arithmetic: 23.3 us -> 2.18 us
  matrix products: 17.6 us -> 0 us
    all_to_all x3 -> x1, waiting for transfers between devices: 70.7 us -> 27.6 us  [shards(): grams = lax.all_to_all(grams, 'zh', split_axis=0, concat_axis=0, tiled=True)]
    scatter x3 -> x0, local copies, waits for them, and re-layouts: 39.7 us -> none  [the longest x1 14.6 us: shards(): jnp.zeros((count,), jnp.bfloat16).at[slot].set(innov)]
    all_to_all x3 -> x1, starting transfers between devices: 45.2 us -> 14 us  [shards(): grams = lax.all_to_all(grams, 'zh', split_axis=0, concat_axis=0, tiled=True)]
    all_to_all x0 -> x1, blocking collectives: none -> 26.9 us  [shards(): lax.all_to_all(sent, ('x', 'zl'), split_axis=0, concat_axis=0, tiled=True)]
    pallas_call x0 -> x4, Pallas kernels: none -> 26.6 us  [the longest x1 7.69 us: route(): pl.pallas_call(route_kernel, grid=(GROUP,), in_specs=[whole((1, OBS)), wh...]
    another operation x3 -> x1, other arithmetic: 18.5 us -> 0.95 us  [shards(): line = jnp.stack([even, own, odd])]
    dot_general x29 -> x0, matrix products: 17.6 us -> none  [the longest x8 3.63 us: node_transform(): jnp.dot(root, current_iterate, precision=lax.Precision.HIGHEST)]
  transfers between devices with their start and end apart: 7 -> 5, of which waited for: 5 -> 3; matrix products, arithmetic and copies ran while one was open for 12% -> 1% of each run, Pallas kernels for 0% -> 0%
where the time goes in v1:
time: 129 us; the launch traced here: 128 us
  waiting for transfers between devices  40.9 us (32%)
  starting transfers between devices  29.4 us (23%)
  blocking collectives  26.9 us (21%)
  Pallas kernels  26.6 us (21%)
  local copies, waits for them, and re-layouts  2.33 us (2%)
  other arithmetic  2.18 us (2%)
    all_to_all x1, waiting for transfers between devices, shards(): grams = lax.all_to_all(grams, 'zh', split_axis=0, concat_axis=0, tiled=True)  27.6 us
    all_to_all x1, blocking collectives, shards(): lax.all_to_all(sent, ('x', 'zl'), split_axis=0, concat_axis=0, tiled=True)  26.9 us
    ppermute x4, starting transfers between devices, swap(): return (lax.ppermute(block, axes, even), lax.ppermute(block, axes, odd))  15.4 us
    all_to_all x1, starting transfers between devices, shards(): grams = lax.all_to_all(grams, 'zh', split_axis=0, concat_axis=0, tiled=True)  14 us
    ppermute x4, waiting for transfers between devices, swap(): return (lax.ppermute(block, axes, even), lax.ppermute(block, axes, odd))  13.3 us
    pallas_call x1, Pallas kernels, route(): pl.pallas_call(route_kernel, grid=(GROUP,), in_specs=[whole((1, OBS)), wh...  7.69 us
    pallas_call x1, Pallas kernels, node_transform(): pl.pallas_call(newton_kernel, out_shape=jax.ShapeDtypeStruct((K, K), BF16...  6.83 us
    pallas_call x1, Pallas kernels, partial_grams(): pl.pallas_call(gram_kernel, grid=(HIGH,), in_specs=[pl.BlockSpec((GROUP,...  6.27 us
  transfers between devices with their start and end apart: 5, of which 3 were waited for; matrix products, arithmetic and copies ran while one was open for 1% of the time, Pallas kernels for 0%

profile of v1, /device:TPU:25, one launch (start us, length us, event | category | flops | bytes accessed | tf_op | source)
XLA Modules:
  0.0 128.4 jit_solution(16041767199838011904)
XLA Ops:
  0.0 7.7 %route.1 = bf16[8,400,256]{2,1,0:T(8,128)(2,1)} custom-call(s32[1,2048]{1,0:T(1,128)} %bitcast.15, bf16[1,2048]{1,0:T(2,128)(2,1)} %weight_ref.1, bf16[1,2048]{1,0:T(2,128)(2,1)} %innov_ref.1, bf16[2048,256]{1,0:T(8,128)(2,1)} %bitcast.12), custom_call_target="tpu_custom_call" | custom-call | tf_op jit(solution)/shard_map/route/pallas_call | solution.py:75
  7.7 26.9 %all_to_all.10.obs_ref.side_ref = bf16[8,400,256]{2,1,0:T(8,128)(2,1)} all-to-all(bf16[8,400,256]{2,1,0:T(8,128)(2,1)} %route.1), channel_id=1, replica_groups=mesh['x'=4,'zh'=8,'zl'=2,'y'=4,'c'=2] {'x','zl'}, dimensions={0} | all-to-all | bytes 3276800 | tf_op jit(solution)/shard_map/all_to_all | solution.py:229
  34.5 0.0 copy-start.3
  34.5 6.3 %gram.1 = bf16[8,264,128]{2,1,0:T(8,128)(2,1)} custom-call(bf16[8,400,256]{2,1,0:T(8,128)(2,1)} %all_to_all.10.obs_ref.side_ref, bf16[8,400,256]{2,1,0:T(8,128)(2,1)} %all_to_all.10.obs_ref.side_ref), custom_call_target="tpu_custom_call" | custom-call | tf_op jit(solution)/shard_map/gram/pallas_call | solution.py:122
  40.8 0.0 copy-start.4
  40.8 14.0 %all-to-all-start.1 = ((bf16[8,264,128]{2,1,0:T(8,128)(2,1)}), bf16[8,264,128]{2,1,0:T(8,128)(2,1)S(1)}, u32[]{:S(2)}, u32[]{:S(2)}) async-start(bf16[8,264,128]{2,1,0:T(8,128)(2,1)} %gram.1), calls=%async_computation.1 | async-start | bytes 1081344 | tf_op jit(solution)/shard_map/all_to_all | solution.py:231
  54.9 0.0 copy-done.3
  54.9 0.1 div.20
  55.0 0.1 rem.52
  55.1 27.6 %all-to-all-done.1.got_ref = bf16[8,264,128]{2,1,0:T(8,128)(2,1)S(1)} async-done(((bf16[8,264,128]{2,1,0:T(8,128)(2,1)}), bf16[8,264,128]{2,1,0:T(8,128)(2,1)S(1)}, u32[]{:S(2)}, u32[]{:S(2)}) %all-to-all-start.1) | async-done | bytes 540704 | tf_op jit(solution)/shard_map/all_to_all | solution.py:231
  82.6 0.0 copy-start
  82.6 0.8 copy-done
  83.4 6.8 %newton.1 = bf16[256,256]{1,0:T(8,128)(2,1)} custom-call(bf16[8,264,128]{2,1,0:T(8,128)(2,1)} %copy-done), custom_call_target="tpu_custom_call" | custom-call | tf_op jit(solution)/shard_map/newton/pallas_call | solution.py:181
  90.3 0.0 copy-start.2
  90.3 2.0 %collective-permute-start = (bf16[256,256]{1,0:T(8,128)(2,1)}, bf16[256,256]{1,0:T(8,128)(2,1)S(1)}, u32[]{:S(2)}, u32[]{:S(2)}) collective-permute-start(bf16[256,256]{1,0:T(8,128)(2,1)} %newton.1), channel_id=1, source_target_pairs={{0,8},{8,0},{16,24},{24,16},{32,40},{40,32},{48,56},{56,48},{64,72... | collective-permute-start | bytes 393224 | tf_op jit(solution)/shard_map/ppermute | solution.py:224
  92.3 3.9 %collective-permute-start.1 = (bf16[256,256]{1,0:T(8,128)(2,1)}, bf16[256,256]{1,0:T(8,128)(2,1)S(1)}, u32[]{:S(2)}, u32[]{:S(2)}) collective-permute-start(bf16[256,256]{1,0:T(8,128)(2,1)} %newton.1), channel_id=1, source_target_pairs={{0,504},{8,16},{16,8},{24,32},{32,24},{40,48},{48,40},{56,64},{64,... | collective-permute-start | bytes 393224 | tf_op jit(solution)/shard_map/ppermute | solution.py:224
  96.2 0.1 ne.38
  96.3 0.0 copy-done.4
  96.3 0.1 reshape.23
  96.4 0.1 div.21
  96.5 0.0 collective-permute-done
  96.5 5.0 %collective-permute-done.1 = bf16[256,256]{1,0:T(8,128)(2,1)S(1)} collective-permute-done((bf16[256,256]{1,0:T(8,128)(2,1)}, bf16[256,256]{1,0:T(8,128)(2,1)S(1)}, u32[]{:S(2)}, u32[]{:S(2)}) %collective-permute-start.1) | collective-permute-done | bytes 131104 | tf_op jit(solution)/shard_map/ppermute | solution.py:224
  101.6 0.9 pad_maximum_fusion
  102.5 7.5 %collective-permute-start.2 = (bf16[3,256,256]{2,1,0:T(8,128)(2,1)S(1)}, bf16[3,256,256]{2,1,0:T(8,128)(2,1)S(1)}, u32[]{:S(2)}, u32[]{:S(2)}) collective-permute-start(bf16[3,256,256]{2,1,0:T(8,128)(2,1)S(1)} %pad_maximum_fusion), channel_id=1, source_target_pairs={{0,1},{1,0},{2,3},{3,2},{4,5},{5,4},{6,7},{7,6},{8,9},{9,8},{10,11... | collective-permute-start | bytes 1179656 | tf_op jit(solution)/shard_map/ppermute | solution.py:224
  110.0 0.6 broadcast_divide_fusion.1.share_ref
  110.7 0.6 fusion.1.slot_ref
  111.2 1.9 %collective-permute-start.3 = (bf16[3,256,256]{2,1,0:T(8,128)(2,1)S(1)}, bf16[3,256,256]{2,1,0:T(8,128)(2,1)S(1)}, u32[]{:S(2)}, u32[]{:S(2)}) collective-permute-start(bf16[3,256,256]{2,1,0:T(8,128)(2,1)S(1)} %pad_maximum_fusion), channel_id=1, source_target_pairs={{0,7},{1,2},{2,1},{3,4},{4,3},{5,6},{6,5},{7,0},{8,15},{9,10},{10,... | collective-permute-start | bytes 1179656 | tf_op jit(solution)/shard_map/ppermute | solution.py:224
  113.2 0.0 collective-permute-done.2
  113.2 0.0 copy-done.2
  113.3 8.3 %collective-permute-done.3 = bf16[3,256,256]{2,1,0:T(8,128)(2,1)S(1)} collective-permute-done((bf16[3,256,256]{2,1,0:T(8,128)(2,1)S(1)}, bf16[3,256,256]{2,1,0:T(8,128)(2,1)S(1)}, u32[]{:S(2)}, u32[]{:S(2)}) %collective-permute-start.3) | collective-permute-done | bytes 393248 | tf_op jit(solution)/shard_map/ppermute | solution.py:224
  121.6 0.0 copy-start.1
  121.6 1.0 copy-done.1
  122.6 5.8 %analysis.1 = bf16[16,128,256]{2,1,0:T(8,128)(2,1)} custom-call(s32[4,16]{1,0:T(4,128)} %fusion.1.slot_ref, f32[4,16]{1,0:T(4,128)} %broadcast_divide_fusion.1.share_ref, bf16[9,256,256]{2,1,0:T(8,128)(2,1)} %copy-done.1, bf16[16,128,256]{2,1,0:T(8,128)(2,1)} %bitcast.11), custom_call_target="tpu_custom_call" | custom-call | tf_op jit(solution)/shard_map/analysis/pallas_call | solution.py:208
  (8 shorter events, 0.1 us)
Async XLA Ops:
  34.5 20.3 %copy-start.3 = (s32[4,2,8]{2,1,0:T(2,128)S(1)}, s32[4,2,8]{2,1,0:T(2,128)}, u32[]{:S(2)}) copy-start(s32[4,2,8]{2,1,0:T(2,128)} %param.12) | copy-start | bytes 772
  40.8 55.5 %copy-start.4 = (f32[4,2,8]{2,1,0:T(2,128)S(1)}, f32[4,2,8]{2,1,0:T(2,128)}, u32[]{:S(2)}) copy-start(f32[4,2,8]{2,1,0:T(2,128)} %param.13) | copy-start | bytes 772
  40.8 41.8 %all-to-all-start.1 = ((bf16[8,264,128]{2,1,0:T(8,128)(2,1)}), bf16[8,264,128]{2,1,0:T(8,128)(2,1)S(1)}, u32[]{:S(2)}, u32[]{:S(2)}) async-start(bf16[8,264,128]{2,1,0:T(8,128)(2,1)} %gram.1), calls=%async_computation.1 | async-start | bytes 1081344 | tf_op jit(solution)/shard_map/all_to_all | solution.py:231
  82.6 0.8 copy-start
  90.3 23.0 %copy-start.2 = (bf16[256,256]{1,0:T(8,128)(2,1)S(1)}, bf16[256,256]{1,0:T(8,128)(2,1)}, u32[]{:S(2)}) copy-start(bf16[256,256]{1,0:T(8,128)(2,1)} %newton.1) | copy-start | bytes 393220
  90.3 6.2 %collective-permute-start = (bf16[256,256]{1,0:T(8,128)(2,1)}, bf16[256,256]{1,0:T(8,128)(2,1)S(1)}, u32[]{:S(2)}, u32[]{:S(2)}) collective-permute-start(bf16[256,256]{1,0:T(8,128)(2,1)} %newton.1), channel_id=1, source_target_pairs={{0,8},{8,0},{16,24},{24,16},{32,40},{40,32},{48,56},{56,48},{64,72... | collective-permute-start | bytes 393224 | tf_op jit(solution)/shard_map/ppermute | solution.py:224
  92.3 9.2 %collective-permute-start.1 = (bf16[256,256]{1,0:T(8,128)(2,1)}, bf16[256,256]{1,0:T(8,128)(2,1)S(1)}, u32[]{:S(2)}, u32[]{:S(2)}) collective-permute-start(bf16[256,256]{1,0:T(8,128)(2,1)} %newton.1), channel_id=1, source_target_pairs={{0,504},{8,16},{16,8},{24,32},{32,24},{40,48},{48,40},{56,64},{64,... | collective-permute-start | bytes 393224 | tf_op jit(solution)/shard_map/ppermute | solution.py:224
  102.5 10.6 %collective-permute-start.2 = (bf16[3,256,256]{2,1,0:T(8,128)(2,1)S(1)}, bf16[3,256,256]{2,1,0:T(8,128)(2,1)S(1)}, u32[]{:S(2)}, u32[]{:S(2)}) collective-permute-start(bf16[3,256,256]{2,1,0:T(8,128)(2,1)S(1)} %pad_maximum_fusion), channel_id=1, source_target_pairs={{0,1},{1,0},{2,3},{3,2},{4,5},{5,4},{6,7},{7,6},{8,9},{9,8},{10,11... | collective-permute-start | bytes 1179656 | tf_op jit(solution)/shard_map/ppermute | solution.py:224
  111.2 10.3 %collective-permute-start.3 = (bf16[3,256,256]{2,1,0:T(8,128)(2,1)S(1)}, bf16[3,256,256]{2,1,0:T(8,128)(2,1)S(1)}, u32[]{:S(2)}, u32[]{:S(2)}) collective-permute-start(bf16[3,256,256]{2,1,0:T(8,128)(2,1)S(1)} %pad_maximum_fusion), channel_id=1, source_target_pairs={{0,7},{1,2},{2,1},{3,4},{4,3},{5,6},{6,5},{7,0},{8,15},{9,10},{10,... | collective-permute-start | bytes 1179656 | tf_op jit(solution)/shard_map/ppermute | solution.py:224
  121.6 1.0 copy-start.1

commit v2 on v1

--- a/solution.py
+++ b/solution.py
@@ -84,51 +84,58 @@
             pltpu.VMEM((NODES, K), F32),
         ],
         name="route",
+        compiler_params=pltpu.CompilerParams(vmem_limit_bytes=40 << 20),
     )(node, weight, innov, pert)
+
+
+PER = 2
 
 
 def gram_kernel(obs_ref, side_ref, out_ref):
     step = pl.program_id(0)
-    obs = obs_ref[...].reshape(GROUP * CAP, K)
-    gram = lax.dot_general(obs, obs, (((0,), (0,)), ((), ())), preferred_element_type=F32)
-    first, cross, last = gram[:HALF, :HALF], gram[:HALF, HALF:], gram[HALF:, HALF:]
     low, high = iota((HALF, HALF), 0), iota((HALF, HALF), 1)
     eye = low == high
-    first_diag = jnp.sum(jnp.where(eye, first, 0.0), 0, keepdims=True)
-    last_diag = jnp.sum(jnp.where(eye, last, 0.0), 0, keepdims=True)
+    keep = low <= high
+    rest = lambda v: v - v.astype(WIRE).astype(F32)
     sides = jnp.sum(side_ref[...].astype(F32), 0)
-    mine = iota((16, K), 0) % HIGH == step
-    rhs = jnp.sum(jnp.where(mine, sides, 0.0), 0, keepdims=True)
-    out_ref[0, :HALF, :] = jnp.where(low <= high, first, last).astype(WIRE)
-    out_ref[0, HALF:K, :] = cross.astype(WIRE)
-    rest = lambda v: v - v.astype(WIRE).astype(F32)
-    extra = jnp.concatenate(
-        [
-            last_diag,
-            rest(last_diag),
-            rest(first_diag),
-            rhs[:, :HALF],
-            rhs[:, HALF:],
-            rest(rhs[:, :HALF]),
-            rest(rhs[:, HALF:]),
-            jnp.zeros((1, HALF), F32),
-        ],
-        0,
-    )
-    out_ref[0, K:, :] = extra.astype(WIRE)
+    name = iota((16, K), 0) % HIGH
+    for n in range(PER):
+        obs = obs_ref[:, n * CAP : (n + 1) * CAP, :].reshape(GROUP * CAP, K)
+        gram = lax.dot_general(obs, obs, (((0,), (0,)), ((), ())), preferred_element_type=F32)
+        first, cross, last = gram[:HALF, :HALF], gram[:HALF, HALF:], gram[HALF:, HALF:]
+        first_diag = jnp.sum(jnp.where(eye, first, 0.0), 0, keepdims=True)
+        last_diag = jnp.sum(jnp.where(eye, last, 0.0), 0, keepdims=True)
+        rhs = jnp.sum(jnp.where(name == step * PER + n, sides, 0.0), 0, keepdims=True)
+        out_ref[n, :HALF, :] = jnp.where(keep, first, last).astype(WIRE)
+        out_ref[n, HALF:K, :] = cross.astype(WIRE)
+        extra = jnp.concatenate(
+            [
+                last_diag,
+                rest(last_diag),
+                rest(first_diag),
+                rhs[:, :HALF],
+                rhs[:, HALF:],
+                rest(rhs[:, :HALF]),
+                rest(rhs[:, HALF:]),
+                jnp.zeros((1, HALF), F32),
+            ],
+            0,
+        )
+        out_ref[n, K:, :] = extra.astype(WIRE)
 
 
 def partial_grams(got):
     return pl.pallas_call(
         gram_kernel,
-        grid=(HIGH,),
+        grid=(HIGH // PER,),
         in_specs=[
-            pl.BlockSpec((GROUP, CAP, K), lambda h: (0, h, 0)),
+            pl.BlockSpec((GROUP, PER * CAP, K), lambda h: (0, h, 0)),
             pl.BlockSpec((GROUP, 16, K), lambda h: (0, HIGH * CAP // 16, 0)),
         ],
-        out_specs=pl.BlockSpec((1, PACKED, HALF), lambda h: (h, 0, 0)),
+        out_specs=pl.BlockSpec((PER, PACKED, HALF), lambda h: (h, 0, 0)),
         out_shape=jax.ShapeDtypeStruct((HIGH, PACKED, HALF), WIRE),
         name="gram",
+        compiler_params=pltpu.CompilerParams(vmem_limit_bytes=16 << 20),
     )(got, got)
 
 
@@ -163,13 +170,19 @@
     identity = (iota((K, K), 0) == iota((K, K), 1)).astype(F32)
     error = gram / total
     root = None
-    for step in range(NEWTON_STEPS):
-        middle = 1.5 * identity - 0.5 * error
-        middle_parts = split(middle)
-        root = middle if step == 0 else dot3(split(root), middle_parts)
-        if step < NEWTON_STEPS - 1:
-            error = dot3(split(error), middle_parts)
-            error = dot3(split(error), middle_parts)
+    for step in range(NEWTON_STEPS - 1):
+        top, rest = split(error)
+        half = (0.5 * error).astype(BF16)
+        dot = lambda u: jnp.dot(u, half, preferred_element_type=F32)
+        if step == 0:
+            root = 1.5 * identity - half.astype(F32)
+        else:
+            root_top, root_rest = split(root)
+            root = 1.5 * root - (dot(root_top) + dot(root_rest))
+        error = 1.5 * error - (dot(top) + dot(rest))
+        top, rest = split(error)
+        error = 1.5 * error - (dot(top) + dot(rest))
+    root = 1.5 * root - 0.5 * dot3(split(root), split(error))
     once = jnp.dot(
         jnp.broadcast_to(rhs, (8, K)), root, precision=lax.Precision.HIGHEST, preferred_element_type=F32
     )[:1]
@@ -182,16 +195,28 @@
         newton_kernel,
         out_shape=jax.ShapeDtypeStruct((K, K), BF16),
         name="newton",
+        compiler_params=pltpu.CompilerParams(vmem_limit_bytes=12 << 20),
     )(got)
 
 
-def analysis_kernel(slot_ref, share_ref, table_ref, state_ref, out_ref):
+def analysis_kernel(slot_ref, share_ref, flip_ref, table_ref, state_ref, out_ref):
     step = pl.program_id(0)
+    flip_x, flip_y = flip_ref[0], flip_ref[1]
     for n in range(COLS):
         column = step * COLS + n
-        blend = share_ref[0, column] * table_ref[slot_ref[0, column]].astype(F32)
-        for q in range(1, 4):
-            blend += share_ref[q, column] * table_ref[slot_ref[q, column]].astype(F32)
+        cx, cy = column // CY, column % CY
+        total = 0.0
+        blend = None
+        for q in range(4):
+            slot = slot_ref[q, cx, cy]
+            ox, oy = slot // 3, slot % 3
+            ox = jnp.where(flip_x == 1, ox, 2 - ox)
+            oy = jnp.where(flip_y == 1, oy, 2 - oy)
+            share = share_ref[q, cx, cy]
+            total += share
+            term = share * table_ref[oy * 3 + ox].astype(F32)
+            blend = term if q == 0 else blend + term
+        blend = blend / jnp.full((1, 1), total, F32)
         state = state_ref[n].astype(F32)
         mean = jnp.mean(state, -1, keepdims=True)
         anomaly = (state - mean).astype(BF16)
@@ -199,23 +224,26 @@
         out_ref[n] = (mean + update).astype(BF16)
 
 
+CX = 2
+CY = 8
 COLS = 4
 
 
-def analyse(slots, share, table, state):
+def analyse(slots, share, flips, table, state):
     columns, levels, width = state.shape
     block = pl.BlockSpec((COLS, levels, width), lambda f, *_: (f, 0, 0))
     return pl.pallas_call(
         analysis_kernel,
         grid_spec=pltpu.PrefetchScalarGridSpec(
-            num_scalar_prefetch=2,
+            num_scalar_prefetch=3,
             grid=(columns // COLS,),
             in_specs=[pl.BlockSpec((9, K, K), lambda f, *_: (0, 0, 0)), block],
             out_specs=block,
         ),
         out_shape=jax.ShapeDtypeStruct(state.shape, BF16),
         name="analysis",
-    )(slots, share, table, state)
+        compiler_params=pltpu.CompilerParams(vmem_limit_bytes=16 << 20),
+    )(slots, share, flips, table, state)
 
 
 def swap(block, axes, count):
@@ -234,18 +262,9 @@
     line = jnp.stack([even, own, odd])
     even, odd = swap(line, GY, 8)
     table = jnp.concatenate([even, line, odd])
-    columns = members.shape[0] * members.shape[1]
-    slots = neighbour_slot.reshape(4, columns)
-    share = interp_weight.reshape(4, columns)
-    share = share / jnp.sum(share, 0)
-
-    def place(offset, axes):
-        flip = lax.axis_index(axes) % 2 == 1
-        return jnp.where(flip, offset, 2 - offset)
-
-    slots = place(slots % 3, GY) * 3 + place(slots // 3, GX)
-    state = members.reshape(columns, *members.shape[2:])
-    return analyse(slots, share, table, state).reshape(members.shape)
+    flips = jnp.stack([lax.axis_index(GX) % 2, lax.axis_index(GY) % 2]).astype(jnp.int32)
+    state = members.reshape(CX * CY, *members.shape[2:])
+    return analyse(neighbour_slot, interp_weight, flips, table, state).reshape(members.shape)
 
 
 def solution(mesh):

time: 129 us -> 117 us (0.907)
  blocking collectives: 26.9 us -> 68.6 us
  waiting for transfers between devices: 40.9 us -> 11.7 us
  starting transfers between devices: 29.4 us -> 16.7 us
  Pallas kernels: 26.6 us -> 15.6 us
  other arithmetic: 2.18 us -> 0.12 us
    all_to_all x0 -> x1, blocking collectives: none -> 42 us  [shards(): grams = lax.all_to_all(grams, 'zh', split_axis=0, concat_axis=0, tiled=True)]
    all_to_all x1 -> x0, waiting for transfers between devices: 27.6 us -> none  [shards(): grams = lax.all_to_all(grams, 'zh', split_axis=0, concat_axis=0, tiled=True)]
    all_to_all x1 -> x0, starting transfers between devices: 14 us -> none  [shards(): grams = lax.all_to_all(grams, 'zh', split_axis=0, concat_axis=0, tiled=True)]
    pallas_call x1, Pallas kernels: 6.27 us -> 1.69 us  [partial_grams(): pl.pallas_call(gram_kernel, grid=(HIGH // PER,), in_specs=[pl.BlockSpec((...]
    pallas_call x1, Pallas kernels: 6.83 us -> 4.23 us  [node_transform(): pl.pallas_call(newton_kernel, out_shape=jax.ShapeDtypeStruct((K, K), BF16...]
    pallas_call x1, Pallas kernels: 7.69 us -> 5.48 us  [route(): pl.pallas_call(route_kernel, grid=(GROUP,), in_specs=[whole((1, OBS)), wh...]
    ppermute x4, waiting for transfers between devices: 13.3 us -> 11.7 us  [swap(): return (lax.ppermute(block, axes, even), lax.ppermute(block, axes, odd))]
    pallas_call x1, Pallas kernels: 5.77 us -> 4.19 us  [analyse(): pl.pallas_call(analysis_kernel, grid_spec=pltpu.PrefetchScalarGridSpec(nu...]
  transfers between devices with their start and end apart: 5 -> 4, of which waited for: 3 -> 2; matrix products, arithmetic and copies ran while one was open for 1% -> 0% of each run, Pallas kernels for 0% -> 0%
where the time goes in v2:
time: 117 us; the launch traced here: 116 us
  blocking collectives  68.6 us (59%)
  starting transfers between devices  16.7 us (14%)
  Pallas kernels  15.6 us (13%)
  waiting for transfers between devices  11.7 us (10%)
  local copies, waits for them, and re-layouts  3.41 us (3%)
    all_to_all x1, blocking collectives, shards(): grams = lax.all_to_all(grams, 'zh', split_axis=0, concat_axis=0, tiled=True)  42 us
    all_to_all x1, blocking collectives, shards(): lax.all_to_all(sent, ('x', 'zl'), split_axis=0, concat_axis=0, tiled=True)  26.6 us
    ppermute x4, starting transfers between devices, swap(): return (lax.ppermute(block, axes, even), lax.ppermute(block, axes, odd))  16.7 us
    ppermute x4, waiting for transfers between devices, swap(): return (lax.ppermute(block, axes, even), lax.ppermute(block, axes, odd))  11.7 us
    pallas_call x1, Pallas kernels, route(): pl.pallas_call(route_kernel, grid=(GROUP,), in_specs=[whole((1, OBS)), wh...  5.48 us
    pallas_call x1, Pallas kernels, node_transform(): pl.pallas_call(newton_kernel, out_shape=jax.ShapeDtypeStruct((K, K), BF16...  4.23 us
    pallas_call x1, Pallas kernels, analyse(): pl.pallas_call(analysis_kernel, grid_spec=pltpu.PrefetchScalarGridSpec(nu...  4.19 us
    unnamed x18, local copies, waits for them, and re-layouts  3.38 us
  transfers between devices with their start and end apart: 4, of which 2 were waited for; matrix products, arithmetic and copies ran while one was open for 0% of the time, Pallas kernels for 0%

profile of v2, /device:TPU:25, one launch (start us, length us, event | category | flops | bytes accessed | tf_op | source)
XLA Modules:
  0.0 116.3 jit_solution(14512421128826732725)
XLA Ops:
  0.0 0.0 copy-start.1
  0.0 1.2 %copy-done.1 = bf16[1,2048,256]{2,1,0:T(8,128)(2,1)S(1)} copy-done((bf16[1,2048,256]{2,1,0:T(8,128)(2,1)S(1)}, bf16[1,2048,256]{2,1,0:T(8,128)(2,1)}, u32[]{:S(2)}) %copy-start.1) | copy-done | bytes 1048600
  1.2 0.0 copy-start.2
  1.2 0.7 copy-done.2
  1.9 0.0 copy-start.3
  1.9 0.7 copy-done.3
  2.6 0.0 copy-start.4
  2.6 0.7 copy-done.4
  3.3 5.5 %route.1 = bf16[8,400,256]{2,1,0:T(8,128)(2,1)S(1)} custom-call(s32[1,2048]{1,0:T(1,128)S(1)} %bitcast.15, bf16[1,2048]{1,0:T(2,128)(2,1)S(1)} %copy-done.3, bf16[1,2048]{1,0:T(2,128)(2,1)S(1)} %copy-done.4, bf16[2048,256]{1,0:T(8,128)(2,1)S(1)} %bitcast.14), custom_call_target="tpu_custom_call" | custom-call | tf_op jit(solution)/shard_map/route/pallas_call | solution.py:75
  8.8 26.6 %all_to_all.10.obs_ref.side_ref = bf16[8,400,256]{2,1,0:T(8,128)(2,1)S(1)} all-to-all(bf16[8,400,256]{2,1,0:T(8,128)(2,1)S(1)} %route.1), channel_id=1, replica_groups=mesh['x'=4,'zh'=8,'zl'=2,'y'=4,'c'=2] {'x','zl'}, dimensions={0} | all-to-all | bytes 3276800 | tf_op jit(solution)/shard_map/all_to_all | solution.py:257
  35.4 1.7 %gram.1 = bf16[8,264,128]{2,1,0:T(8,128)(2,1)S(1)} custom-call(bf16[8,400,256]{2,1,0:T(8,128)(2,1)S(1)} %all_to_all.10.obs_ref.side_ref, bf16[8,400,256]{2,1,0:T(8,128)(2,1)S(1)} %all_to_all.10.obs_ref.side_ref), custom_call_target="tpu_custom_call" | custom-call | tf_op jit(solution)/shard_map/gram/pallas_call | solution.py:128
  37.1 42.0 %all_to_all.11.got_ref = bf16[8,264,128]{2,1,0:T(8,128)(2,1)S(1)} all-to-all(bf16[8,264,128]{2,1,0:T(8,128)(2,1)S(1)} %gram.1), channel_id=1, replica_groups=mesh['x'=4,'zh'=8,'zl'=2,'y'=4,'c'=2] {'zh'}, dimensions={0} | all-to-all | bytes 1081344 | tf_op jit(solution)/shard_map/all_to_all | solution.py:259
  79.1 4.2 %newton.1 = bf16[256,256]{1,0:T(8,128)(2,1)S(1)} custom-call(bf16[8,264,128]{2,1,0:T(8,128)(2,1)S(1)} %all_to_all.11.got_ref), custom_call_target="tpu_custom_call" | custom-call | tf_op jit(solution)/shard_map/newton/pallas_call | solution.py:194
  83.3 8.1 %collective-permute-start.1 = (bf16[256,256]{1,0:T(8,128)(2,1)S(1)}, bf16[256,256]{1,0:T(8,128)(2,1)S(1)}, u32[]{:S(2)}, u32[]{:S(2)}) collective-permute-start(bf16[256,256]{1,0:T(8,128)(2,1)S(1)} %newton.1), channel_id=1, source_target_pairs={{0,504},{8,16},{16,8},{24,32},{32,24},{40,48},{48,40},{56,64},{64,... | collective-permute-start | bytes 393224 | tf_op jit(solution)/shard_map/ppermute | solution.py:252
  91.4 2.6 %collective-permute-start = (bf16[256,256]{1,0:T(8,128)(2,1)S(1)}, bf16[256,256]{1,0:T(8,128)(2,1)S(1)}, u32[]{:S(2)}, u32[]{:S(2)}) collective-permute-start(bf16[256,256]{1,0:T(8,128)(2,1)S(1)} %newton.1), channel_id=1, source_target_pairs={{0,8},{8,0},{16,24},{24,16},{32,40},{40,32},{48,56},{56,48},{64,72... | collective-permute-start | bytes 393224 | tf_op jit(solution)/shard_map/ppermute | solution.py:252
  94.0 0.0 collective-permute-done.1
  94.0 3.4 %collective-permute-done = bf16[256,256]{1,0:T(8,128)(2,1)S(1)} collective-permute-done((bf16[256,256]{1,0:T(8,128)(2,1)S(1)}, bf16[256,256]{1,0:T(8,128)(2,1)S(1)}, u32[]{:S(2)}, u32[]{:S(2)}) %collective-permute-start) | collective-permute-done | bytes 131104 | tf_op jit(solution)/shard_map/ppermute | solution.py:252
  97.5 4.1 %collective-permute-start.2 = (bf16[3,256,256]{2,1,0:T(8,128)(2,1)S(1)}, bf16[3,256,256]{2,1,0:T(8,128)(2,1)S(1)}, u32[]{:S(2)}, u32[]{:S(2)}) collective-permute-start(bf16[3,256,256]{2,1,0:T(8,128)(2,1)S(1)} %pad_maximum_fusion), channel_id=1, source_target_pairs={{0,1},{1,0},{2,3},{3,2},{4,5},{5,4},{6,7},{7,6},{8,9},{9,8},{10,11... | collective-permute-start | bytes 1179656 | tf_op jit(solution)/shard_map/ppermute | solution.py:252
  101.6 0.1 pad_add_fusion.flip_ref
  101.6 0.0 copy-start
  101.6 0.0 copy-start.5
  101.6 0.0 copy-start.6
  101.6 2.0 %collective-permute-start.3 = (bf16[3,256,256]{2,1,0:T(8,128)(2,1)S(1)}, bf16[3,256,256]{2,1,0:T(8,128)(2,1)S(1)}, u32[]{:S(2)}, u32[]{:S(2)}) collective-permute-start(bf16[3,256,256]{2,1,0:T(8,128)(2,1)S(1)} %pad_maximum_fusion), channel_id=1, source_target_pairs={{0,7},{1,2},{2,1},{3,4},{4,3},{5,6},{6,5},{7,0},{8,15},{9,10},{10,... | collective-permute-start | bytes 1179656 | tf_op jit(solution)/shard_map/ppermute | solution.py:252
  103.7 0.0 collective-permute-done.2
  103.8 8.3 %collective-permute-done.3 = bf16[3,256,256]{2,1,0:T(8,128)(2,1)S(1)} collective-permute-done((bf16[3,256,256]{2,1,0:T(8,128)(2,1)S(1)}, bf16[3,256,256]{2,1,0:T(8,128)(2,1)S(1)}, u32[]{:S(2)}, u32[]{:S(2)}) %collective-permute-start.3) | collective-permute-done | bytes 393248 | tf_op jit(solution)/shard_map/ppermute | solution.py:252
  112.1 0.0 copy-done
  112.1 0.0 copy-done.5
  112.1 0.0 copy-done.6
  112.1 4.2 %analysis.1 = bf16[16,128,256]{2,1,0:T(8,128)(2,1)} custom-call(s32[4,2,8]{2,1,0:T(2,128)S(1)} %copy-done.5, f32[4,2,8]{2,1,0:T(2,128)S(1)} %copy-done.6, s32[2]{0:T(128)S(1)} %pad_add_fusion.flip_ref, bf16[9,256,256]{2,1,0:T(8,128)(2,1)S(1)} %constant_dynamic-update-slice_fusion.table_ref, bf16[16,128,256]{2,1,0:T(8,128)(2,1)S(1)} %bitcast.13), custom_call_target="tpu_custom_call" | custom-call | tf_op jit(solution)/shard_map/analysis/pallas_call | solution.py:235
  (6 shorter events, 0.1 us)
Async XLA Ops:
  0.0 1.2 %copy-start.1 = (bf16[1,2048,256]{2,1,0:T(8,128)(2,1)S(1)}, bf16[1,2048,256]{2,1,0:T(8,128)(2,1)}, u32[]{:S(2)}) copy-start(bf16[1,2048,256]{2,1,0:T(8,128)(2,1)} %param.8) | copy-start | bytes 3145732
  1.2 0.7 copy-start.2
  1.9 0.7 copy-start.3
  2.6 0.7 copy-start.4
  83.3 10.6 %collective-permute-start.1 = (bf16[256,256]{1,0:T(8,128)(2,1)S(1)}, bf16[256,256]{1,0:T(8,128)(2,1)S(1)}, u32[]{:S(2)}, u32[]{:S(2)}) collective-permute-start(bf16[256,256]{1,0:T(8,128)(2,1)S(1)} %newton.1), channel_id=1, source_target_pairs={{0,504},{8,16},{16,8},{24,32},{32,24},{40,48},{48,40},{56,64},{64,... | collective-permute-start | bytes 393224 | tf_op jit(solution)/shard_map/ppermute | solution.py:252
  91.4 6.0 %collective-permute-start = (bf16[256,256]{1,0:T(8,128)(2,1)S(1)}, bf16[256,256]{1,0:T(8,128)(2,1)S(1)}, u32[]{:S(2)}, u32[]{:S(2)}) collective-permute-start(bf16[256,256]{1,0:T(8,128)(2,1)S(1)} %newton.1), channel_id=1, source_target_pairs={{0,8},{8,0},{16,24},{24,16},{32,40},{40,32},{48,56},{56,48},{64,72... | collective-permute-start | bytes 393224 | tf_op jit(solution)/shard_map/ppermute | solution.py:252
  97.5 6.2 %collective-permute-start.2 = (bf16[3,256,256]{2,1,0:T(8,128)(2,1)S(1)}, bf16[3,256,256]{2,1,0:T(8,128)(2,1)S(1)}, u32[]{:S(2)}, u32[]{:S(2)}) collective-permute-start(bf16[3,256,256]{2,1,0:T(8,128)(2,1)S(1)} %pad_maximum_fusion), channel_id=1, source_target_pairs={{0,1},{1,0},{2,3},{3,2},{4,5},{5,4},{6,7},{7,6},{8,9},{9,8},{10,11... | collective-permute-start | bytes 1179656 | tf_op jit(solution)/shard_map/ppermute | solution.py:252
  101.6 10.5 %copy-start = (bf16[2,8,128,256]{3,2,1,0:T(8,128)(2,1)S(1)}, bf16[2,8,128,256]{3,2,1,0:T(8,128)(2,1)}, u32[]{:S(2)}) copy-start(bf16[2,8,128,256]{3,2,1,0:T(8,128)(2,1)} %param.7) | copy-start | bytes 3145732
  101.6 10.5 %copy-start.5 = (s32[4,2,8]{2,1,0:T(2,128)S(1)}, s32[4,2,8]{2,1,0:T(2,128)}, u32[]{:S(2)}) copy-start(s32[4,2,8]{2,1,0:T(2,128)} %slot_ref.1) | copy-start | bytes 772
  101.6 10.5 %copy-start.6 = (f32[4,2,8]{2,1,0:T(2,128)S(1)}, f32[4,2,8]{2,1,0:T(2,128)}, u32[]{:S(2)}) copy-start(f32[4,2,8]{2,1,0:T(2,128)} %share_ref.1) | copy-start | bytes 772
  101.6 10.4 %collective-permute-start.3 = (bf16[3,256,256]{2,1,0:T(8,128)(2,1)S(1)}, bf16[3,256,256]{2,1,0:T(8,128)(2,1)S(1)}, u32[]{:S(2)}, u32[]{:S(2)}) collective-permute-start(bf16[3,256,256]{2,1,0:T(8,128)(2,1)S(1)} %pad_maximum_fusion), channel_id=1, source_target_pairs={{0,7},{1,2},{2,1},{3,4},{4,3},{5,6},{6,5},{7,0},{8,15},{9,10},{10,... | collective-permute-start | bytes 1179656 | tf_op jit(solution)/shard_map/ppermute | solution.py:252

commit v3 on v2

--- a/solution.py
+++ b/solution.py
@@ -32,11 +32,21 @@
     return lax.broadcasted_iota(jnp.int32, shape, dim)
 
 
-def route_kernel(node_ref, weight_ref, innov_ref, pert_ref, out_ref, rank_ref, scaled_ref, rhs_ref):
+def route_kernel(
+    node_hbm, weight_hbm, innov_hbm, pert_hbm, out_ref,
+    rank_ref, scaled_ref, rhs_ref, node_ref, weight_ref, innov_ref, pert_ref, sems,
+):
     step = pl.program_id(0)
 
     @pl.when(step == 0)
     def _():
+        pairs = (
+            (node_hbm, node_ref), (pert_hbm, pert_ref), (weight_hbm, weight_ref), (innov_hbm, innov_ref),
+        )
+        copies = [pltpu.make_async_copy(a, b, sems.at[i]) for i, (a, b) in enumerate(pairs)]
+        for copy in copies:
+            copy.start()
+        copies[0].wait()
         row = iota((NODES, 1), 0)
         name = (row // 16) * 16 + (row % 8) * 2 + (row // 8) % 2
         onehot = (node_ref[...] == name).astype(F32)
@@ -47,6 +57,8 @@
             count = jnp.dot(part.astype(BF16), upper, preferred_element_type=F32) + carry
             rank_ref[:, b * K : (b + 1) * K] = jnp.where(part > 0, count - 1.0, -1.0)
             carry = count[:, K - 1 : K]
+        for copy in copies[1:]:
+            copy.wait()
         weight = weight_ref[...].astype(F32)
         side = jnp.sqrt(weight)
         side = jnp.concatenate([side[:, k * 128 : (k + 1) * 128] for k in range(OBS // 128)], 0).T
@@ -71,21 +83,25 @@
 
 
 def route(node, weight, innov, pert):
-    whole = lambda shape: pl.BlockSpec(shape, lambda d: (0, 0))
     return pl.pallas_call(
         route_kernel,
         grid=(GROUP,),
-        in_specs=[whole((1, OBS)), whole((1, OBS)), whole((1, OBS)), whole((OBS, K))],
+        in_specs=[pl.BlockSpec(memory_space=pltpu.HBM)] * 4,
         out_specs=pl.BlockSpec((1, ROWS, K), lambda d: (d, 0, 0)),
         out_shape=jax.ShapeDtypeStruct((GROUP, ROWS, K), BF16),
         scratch_shapes=[
             pltpu.VMEM((NODES, OBS), F32),
             pltpu.VMEM((OBS, K), BF16),
             pltpu.VMEM((NODES, K), F32),
+            pltpu.VMEM((1, OBS), jnp.int32),
+            pltpu.VMEM((1, OBS), BF16),
+            pltpu.VMEM((1, OBS), BF16),
+            pltpu.VMEM((OBS, K), BF16),
+            pltpu.SemaphoreType.DMA((4,)),
         ],
         name="route",
         compiler_params=pltpu.CompilerParams(vmem_limit_bytes=40 << 20),
-    )(node, weight, innov, pert)
+    )(*[pltpu.with_memory_space_constraint(v, pltpu.HBM) for v in (node, weight, innov, pert)])
 
 
 PER = 2
@@ -183,17 +199,24 @@
         top, rest = split(error)
         error = 1.5 * error - (dot(top) + dot(rest))
     root = 1.5 * root - 0.5 * dot3(split(root), split(error))
-    once = jnp.dot(
-        jnp.broadcast_to(rhs, (8, K)), root, precision=lax.Precision.HIGHEST, preferred_element_type=F32
-    )[:1]
-    mean_weight = jnp.sum(root * once, 1, keepdims=True) / total
-    out_ref[...] = (mean_weight + jnp.sqrt((K - 1) / total) * root).astype(BF16)
+    once = jnp.sum(root * rhs, 1, keepdims=True) / total
+    mean_weight = jnp.sum(root * once, 0, keepdims=True)
+    root = jnp.sqrt((K - 1) / total) * root
+    first, last = root[:HALF, :HALF], root[HALF:, HALF:]
+    out_ref[:HALF, :] = jnp.where(low < high, first, jnp.where(eye, 0.5 * first, last)).astype(BF16)
+    out_ref[HALF:K, :] = root[:HALF, HALF:].astype(BF16)
+    weights = [mean_weight[:, :HALF], mean_weight[:, HALF:]]
+    tops = [w.astype(BF16).astype(F32) for w in weights]
+    last_diag = jnp.sum(jnp.where(eye, 0.5 * last, 0.0), 0, keepdims=True)
+    rests = [w - t for w, t in zip(weights, tops)]
+    extra = jnp.concatenate([last_diag, *tops, *rests, jnp.zeros((3, HALF), F32)], 0)
+    out_ref[K:, :] = extra.astype(BF16)
 
 
 def node_transform(got):
     return pl.pallas_call(
         newton_kernel,
-        out_shape=jax.ShapeDtypeStruct((K, K), BF16),
+        out_shape=jax.ShapeDtypeStruct((PACKED, HALF), BF16),
         name="newton",
         compiler_params=pltpu.CompilerParams(vmem_limit_bytes=12 << 20),
     )(got)
@@ -202,25 +225,47 @@
 def analysis_kernel(slot_ref, share_ref, flip_ref, table_ref, state_ref, out_ref):
     step = pl.program_id(0)
     flip_x, flip_y = flip_ref[0], flip_ref[1]
+    low, high = iota((HALF, HALF), 0), iota((HALF, HALF), 1)
+    eye = low == high
     for n in range(COLS):
         column = step * COLS + n
         cx, cy = column // CY, column % CY
-        total = 0.0
+        shares = [share_ref[q, cx, cy] for q in range(4)]
+        total = shares[0] + shares[1] + shares[2] + shares[3]
+        scale = 1.0 / jnp.full((1, 1), total, F32)
         blend = None
         for q in range(4):
             slot = slot_ref[q, cx, cy]
             ox, oy = slot // 3, slot % 3
             ox = jnp.where(flip_x == 1, ox, 2 - ox)
             oy = jnp.where(flip_y == 1, oy, 2 - oy)
-            share = share_ref[q, cx, cy]
-            total += share
-            term = share * table_ref[oy * 3 + ox].astype(F32)
+            term = (shares[q] * scale) * table_ref[oy * 3 + ox].astype(F32)
             blend = term if q == 0 else blend + term
-        blend = blend / jnp.full((1, 1), total, F32)
+        mixed, cross, extra = blend[:HALF], blend[HALF:K], blend[K:]
+        upper = jnp.where(low <= high, mixed, 0.0)
+        lower = jnp.where(low > high, mixed, jnp.where(eye, extra[0:1], 0.0))
+        first = extra[1:2] + extra[3:4]
+        last = extra[2:3] + extra[4:5]
+        plain = jnp.concatenate(
+            [
+                jnp.concatenate([upper, cross], 1).astype(BF16),
+                jnp.concatenate([jnp.zeros_like(lower), lower], 1).astype(BF16),
+            ],
+            0,
+        )
+        turned = jnp.concatenate(
+            [
+                jnp.concatenate([upper + first, cross + last], 1).astype(BF16),
+                jnp.concatenate([jnp.broadcast_to(first, lower.shape), lower + last], 1).astype(BF16),
+            ],
+            0,
+        )
         state = state_ref[n].astype(F32)
         mean = jnp.mean(state, -1, keepdims=True)
         anomaly = (state - mean).astype(BF16)
-        update = jnp.dot(anomaly, blend.astype(BF16), preferred_element_type=F32)
+        update = jnp.dot(anomaly, plain, preferred_element_type=F32) + lax.dot_general(
+            anomaly, turned, (((1,), (1,)), ((), ())), preferred_element_type=F32
+        )
         out_ref[n] = (mean + update).astype(BF16)
 
 
@@ -237,7 +282,7 @@
         grid_spec=pltpu.PrefetchScalarGridSpec(
             num_scalar_prefetch=3,
             grid=(columns // COLS,),
-            in_specs=[pl.BlockSpec((9, K, K), lambda f, *_: (0, 0, 0)), block],
+            in_specs=[pl.BlockSpec((9, PACKED, HALF), lambda f, *_: (0, 0, 0)), block],
             out_specs=block,
         ),
         out_shape=jax.ShapeDtypeStruct(state.shape, BF16),

time: 117 us -> 111 us (0.949)
  local copies, waits for them, and re-layouts: 3.41 us -> 0.11 us
  waiting for transfers between devices: 11.7 us -> 9.01 us
    unnamed x18 -> x10, local copies, waits for them, and re-layouts: 3.38 us -> 0.08 us
    ppermute x4, waiting for transfers between devices: 11.7 us -> 9.01 us  [swap(): return (lax.ppermute(block, axes, even), lax.ppermute(block, axes, odd))]
where the time goes in v3:
time: 111 us
  blocking collectives  68.7 us (62%)
  starting transfers between devices  16.6 us (15%)
  Pallas kernels  16.2 us (15%)
  waiting for transfers between devices  9.01 us (8%)
    all_to_all x1, blocking collectives, shards(): grams = lax.all_to_all(grams, 'zh', split_axis=0, concat_axis=0, tiled=True)  42.2 us
    all_to_all x1, blocking collectives, shards(): lax.all_to_all(sent, ('x', 'zl'), split_axis=0, concat_axis=0, tiled=True)  26.6 us
    ppermute x4, starting transfers between devices, swap(): return (lax.ppermute(block, axes, even), lax.ppermute(block, axes, odd))  16.6 us
    ppermute x4, waiting for transfers between devices, swap(): return (lax.ppermute(block, axes, even), lax.ppermute(block, axes, odd))  9.01 us
    pallas_call x1, Pallas kernels, route(): pl.pallas_call(route_kernel, grid=(GROUP,), in_specs=[pl.BlockSpec(memory...  6.57 us
    pallas_call x1, Pallas kernels, analyse(): pl.pallas_call(analysis_kernel, grid_spec=pltpu.PrefetchScalarGridSpec(nu...  4.05 us
    pallas_call x1, Pallas kernels, node_transform(): pl.pallas_call(newton_kernel, out_shape=jax.ShapeDtypeStruct((PACKED, HAL...  3.88 us
  transfers between devices with their start and end apart: 4, of which 2 were waited for; matrix products, arithmetic and copies ran while one was open for 0% of the time, Pallas kernels for 0%

profile of v3, /device:TPU:25, one launch (start us, length us, event | category | flops | bytes accessed | tf_op | source)
XLA Modules:
  0.0 110.9 jit_solution(18023079934107629999)
XLA Ops:
  0.0 6.6 %route.1 = bf16[8,400,256]{2,1,0:T(8,128)(2,1)S(1)} custom-call(s32[1,2048]{1,0:T(1,128)} %bitcast.17, bf16[1,2048]{1,0:T(2,128)(2,1)} %weight_hbm.1, bf16[1,2048]{1,0:T(2,128)(2,1)} %innov_hbm.1, bf16[2048,256]{1,0:T(8,128)(2,1)} %bitcast.14), custom_call_target="tpu_custom_call" | custom-call | tf_op jit(solution)/shard_map/route/pallas_call | solution.py:86
  6.6 26.6 %all_to_all.10.obs_ref.side_ref = bf16[8,400,256]{2,1,0:T(8,128)(2,1)S(1)} all-to-all(bf16[8,400,256]{2,1,0:T(8,128)(2,1)S(1)} %route.1), channel_id=1, replica_groups=mesh['x'=4,'zh'=8,'zl'=2,'y'=4,'c'=2] {'x','zl'}, dimensions={0} | all-to-all | bytes 3276800 | tf_op jit(solution)/shard_map/all_to_all | solution.py:302
  33.1 1.7 %gram.1 = bf16[8,264,128]{2,1,0:T(8,128)(2,1)S(1)} custom-call(bf16[8,400,256]{2,1,0:T(8,128)(2,1)S(1)} %all_to_all.10.obs_ref.side_ref, bf16[8,400,256]{2,1,0:T(8,128)(2,1)S(1)} %all_to_all.10.obs_ref.side_ref), custom_call_target="tpu_custom_call" | custom-call | tf_op jit(solution)/shard_map/gram/pallas_call | solution.py:144
  34.8 0.0 copy-start
  34.9 0.0 copy-start.1
  34.9 0.0 copy-start.2
  34.9 42.2 %all_to_all.11.got_ref = bf16[8,264,128]{2,1,0:T(8,128)(2,1)S(1)} all-to-all(bf16[8,264,128]{2,1,0:T(8,128)(2,1)S(1)} %gram.1), channel_id=1, replica_groups=mesh['x'=4,'zh'=8,'zl'=2,'y'=4,'c'=2] {'zh'}, dimensions={0} | all-to-all | bytes 1081344 | tf_op jit(solution)/shard_map/all_to_all | solution.py:304
  77.0 3.9 %newton.1 = bf16[264,128]{1,0:T(8,128)(2,1)S(1)} custom-call(bf16[8,264,128]{2,1,0:T(8,128)(2,1)S(1)} %all_to_all.11.got_ref), custom_call_target="tpu_custom_call" | custom-call | tf_op jit(solution)/shard_map/newton/pallas_call | solution.py:217
  80.9 8.1 %collective-permute-start.1 = (bf16[264,128]{1,0:T(8,128)(2,1)S(1)}, bf16[264,128]{1,0:T(8,128)(2,1)S(1)}, u32[]{:S(2)}, u32[]{:S(2)}) collective-permute-start(bf16[264,128]{1,0:T(8,128)(2,1)S(1)} %newton.1), channel_id=1, source_target_pairs={{0,504},{8,16},{16,8},{24,32},{32,24},{40,48},{48,40},{56,64},{64,... | collective-permute-start | bytes 202760 | tf_op jit(solution)/shard_map/ppermute | solution.py:297
  89.0 2.6 %collective-permute-start = (bf16[264,128]{1,0:T(8,128)(2,1)S(1)}, bf16[264,128]{1,0:T(8,128)(2,1)S(1)}, u32[]{:S(2)}, u32[]{:S(2)}) collective-permute-start(bf16[264,128]{1,0:T(8,128)(2,1)S(1)} %newton.1), channel_id=1, source_target_pairs={{0,8},{8,0},{16,24},{24,16},{32,40},{40,32},{48,56},{56,48},{64,72... | collective-permute-start | bytes 202760 | tf_op jit(solution)/shard_map/ppermute | solution.py:297
  91.6 0.0 collective-permute-done.1
  91.6 2.8 %collective-permute-done = bf16[264,128]{1,0:T(8,128)(2,1)S(1)} collective-permute-done((bf16[264,128]{1,0:T(8,128)(2,1)S(1)}, bf16[264,128]{1,0:T(8,128)(2,1)S(1)}, u32[]{:S(2)}, u32[]{:S(2)}) %collective-permute-start) | collective-permute-done | bytes 67616 | tf_op jit(solution)/shard_map/ppermute | solution.py:297
  94.3 4.1 %collective-permute-start.2 = (bf16[3,264,128]{2,1,0:T(8,128)(2,1)S(1)}, bf16[3,264,128]{2,1,0:T(8,128)(2,1)S(1)}, u32[]{:S(2)}, u32[]{:S(2)}) collective-permute-start(bf16[3,264,128]{2,1,0:T(8,128)(2,1)S(1)} %pad_maximum_fusion), channel_id=1, source_target_pairs={{0,1},{1,0},{2,3},{3,2},{4,5},{5,4},{6,7},{7,6},{8,9},{9,8},{10,11... | collective-permute-start | bytes 608264 | tf_op jit(solution)/shard_map/ppermute | solution.py:297
  98.4 0.1 pad_add_fusion.flip_ref
  98.5 1.9 %collective-permute-start.3 = (bf16[3,264,128]{2,1,0:T(8,128)(2,1)S(1)}, bf16[3,264,128]{2,1,0:T(8,128)(2,1)S(1)}, u32[]{:S(2)}, u32[]{:S(2)}) collective-permute-start(bf16[3,264,128]{2,1,0:T(8,128)(2,1)S(1)} %pad_maximum_fusion), channel_id=1, source_target_pairs={{0,7},{1,2},{2,1},{3,4},{4,3},{5,6},{6,5},{7,0},{8,15},{9,10},{10,... | collective-permute-start | bytes 608264 | tf_op jit(solution)/shard_map/ppermute | solution.py:297
  100.4 0.0 collective-permute-done.2
  100.5 6.2 %collective-permute-done.3 = bf16[3,264,128]{2,1,0:T(8,128)(2,1)S(1)} collective-permute-done((bf16[3,264,128]{2,1,0:T(8,128)(2,1)S(1)}, bf16[3,264,128]{2,1,0:T(8,128)(2,1)S(1)}, u32[]{:S(2)}, u32[]{:S(2)}) %collective-permute-start.3) | collective-permute-done | bytes 202784 | tf_op jit(solution)/shard_map/ppermute | solution.py:297
  106.8 0.0 copy-done
  106.8 0.0 copy-done.1
  106.8 0.0 copy-done.2
  106.8 4.0 %analysis.1 = bf16[16,128,256]{2,1,0:T(8,128)(2,1)} custom-call(s32[4,2,8]{2,1,0:T(2,128)S(1)} %copy-done.1, f32[4,2,8]{2,1,0:T(2,128)S(1)} %copy-done.2, s32[2]{0:T(128)S(1)} %pad_add_fusion.flip_ref, bf16[9,264,128]{2,1,0:T(8,128)(2,1)S(1)} %constant_dynamic-update-slice_fusion.table_ref, bf16[16,128,256]{2,1,0:T(8,128)(2,1)S(1)} %bitcast.12), custom_call_target="tpu_custom_call" | custom-call | tf_op jit(solution)/shard_map/analysis/pallas_call | solution.py:280
  (6 shorter events, 0.1 us)
Async XLA Ops:
  34.8 72.0 %copy-start = (bf16[2,8,128,256]{3,2,1,0:T(8,128)(2,1)S(1)}, bf16[2,8,128,256]{3,2,1,0:T(8,128)(2,1)}, u32[]{:S(2)}) copy-start(bf16[2,8,128,256]{3,2,1,0:T(8,128)(2,1)} %param.7) | copy-start | bytes 3145732
  34.9 72.0 %copy-start.1 = (s32[4,2,8]{2,1,0:T(2,128)S(1)}, s32[4,2,8]{2,1,0:T(2,128)}, u32[]{:S(2)}) copy-start(s32[4,2,8]{2,1,0:T(2,128)} %slot_ref.1) | copy-start | bytes 772
  34.9 72.0 %copy-start.2 = (f32[4,2,8]{2,1,0:T(2,128)S(1)}, f32[4,2,8]{2,1,0:T(2,128)}, u32[]{:S(2)}) copy-start(f32[4,2,8]{2,1,0:T(2,128)} %share_ref.1) | copy-start | bytes 772
  80.9 10.6 %collective-permute-start.1 = (bf16[264,128]{1,0:T(8,128)(2,1)S(1)}, bf16[264,128]{1,0:T(8,128)(2,1)S(1)}, u32[]{:S(2)}, u32[]{:S(2)}) collective-permute-start(bf16[264,128]{1,0:T(8,128)(2,1)S(1)} %newton.1), channel_id=1, source_target_pairs={{0,504},{8,16},{16,8},{24,32},{32,24},{40,48},{48,40},{56,64},{64,... | collective-permute-start | bytes 202760 | tf_op jit(solution)/shard_map/ppermute | solution.py:297
  89.0 5.3 %collective-permute-start = (bf16[264,128]{1,0:T(8,128)(2,1)S(1)}, bf16[264,128]{1,0:T(8,128)(2,1)S(1)}, u32[]{:S(2)}, u32[]{:S(2)}) collective-permute-start(bf16[264,128]{1,0:T(8,128)(2,1)S(1)} %newton.1), channel_id=1, source_target_pairs={{0,8},{8,0},{16,24},{24,16},{32,40},{40,32},{48,56},{56,48},{64,72... | collective-permute-start | bytes 202760 | tf_op jit(solution)/shard_map/ppermute | solution.py:297
  94.3 6.1 %collective-permute-start.2 = (bf16[3,264,128]{2,1,0:T(8,128)(2,1)S(1)}, bf16[3,264,128]{2,1,0:T(8,128)(2,1)S(1)}, u32[]{:S(2)}, u32[]{:S(2)}) collective-permute-start(bf16[3,264,128]{2,1,0:T(8,128)(2,1)S(1)} %pad_maximum_fusion), channel_id=1, source_target_pairs={{0,1},{1,0},{2,3},{3,2},{4,5},{5,4},{6,7},{7,6},{8,9},{9,8},{10,11... | collective-permute-start | bytes 608264 | tf_op jit(solution)/shard_map/ppermute | solution.py:297
  98.5 8.3 %collective-permute-start.3 = (bf16[3,264,128]{2,1,0:T(8,128)(2,1)S(1)}, bf16[3,264,128]{2,1,0:T(8,128)(2,1)S(1)}, u32[]{:S(2)}, u32[]{:S(2)}) collective-permute-start(bf16[3,264,128]{2,1,0:T(8,128)(2,1)S(1)} %pad_maximum_fusion), channel_id=1, source_target_pairs={{0,7},{1,2},{2,1},{3,4},{4,3},{5,6},{6,5},{7,0},{8,15},{9,10},{10,... | collective-permute-start | bytes 608264 | tf_op jit(solution)/shard_map/ppermute | solution.py:297

commit v4 on v3

--- a/solution.py
+++ b/solution.py
@@ -18,6 +18,7 @@
 HIGH = 8
 GROUP = 8
 CAP = 48
+DESTS = 8
 OBS = 2048
 K = 256
 HALF = 128
@@ -34,7 +35,7 @@
 
 def route_kernel(
     node_hbm, weight_hbm, innov_hbm, pert_hbm, out_ref,
-    rank_ref, scaled_ref, rhs_ref, node_ref, weight_ref, innov_ref, pert_ref, sems,
+    rank_ref, scaled_ref, factor_ref, node_ref, weight_ref, innov_ref, pert_ref, sems,
 ):
     step = pl.program_id(0)
 
@@ -51,48 +52,59 @@
         name = (row // 16) * 16 + (row % 8) * 2 + (row // 8) % 2
         onehot = (node_ref[...] == name).astype(F32)
         upper = (iota((K, K), 0) <= iota((K, K), 1)).astype(BF16)
+        blocks = [onehot[:, b * K : (b + 1) * K] for b in range(OBS // K)]
+        counts = jnp.dot(
+            jnp.concatenate(blocks, 0).astype(BF16), upper, preferred_element_type=F32
+        )
         carry = jnp.zeros((NODES, 1), F32)
-        for b in range(OBS // K):
-            part = onehot[:, b * K : (b + 1) * K]
-            count = jnp.dot(part.astype(BF16), upper, preferred_element_type=F32) + carry
-            rank_ref[:, b * K : (b + 1) * K] = jnp.where(part > 0, count - 1.0, -1.0)
-            carry = count[:, K - 1 : K]
+        for b, block in enumerate(blocks):
+            count = counts[b * NODES : (b + 1) * NODES]
+            rank_ref[:, b * K : (b + 1) * K] = jnp.where(block > 0, count + (carry - 1.0), -1.0)
+            carry += count[:, K - 1 : K]
         for copy in copies[1:]:
             copy.wait()
-        weight = weight_ref[...].astype(F32)
-        side = jnp.sqrt(weight)
+        side = jnp.sqrt(weight_ref[...].astype(F32))
+        factor = onehot * (side * innov_ref[...].astype(F32))
+        top = factor.astype(BF16)
+        factor_ref[:NODES, :] = top
+        factor_ref[NODES:, :] = (factor - top.astype(F32)).astype(BF16)
         side = jnp.concatenate([side[:, k * 128 : (k + 1) * 128] for k in range(OBS // 128)], 0).T
         for k in range(OBS // 128):
             rows = pl.ds(k * 128, 128)
             scaled_ref[rows, :] = (pert_ref[rows, :].astype(F32) * side[:, k : k + 1]).astype(BF16)
-        factor = onehot * (weight * innov_ref[...].astype(F32))
-        top = factor.astype(BF16)
-        rest = (factor - top.astype(F32)).astype(BF16)
-        both = jnp.dot(jnp.concatenate([top, rest], 0), pert_ref[...], preferred_element_type=F32)
-        rhs_ref[...] = both[:NODES] + both[NODES:]
-
-    rank = rank_ref[pl.ds(pl.multiple_of(step * HIGH, HIGH), HIGH), :]
+
+    rows = pl.ds(pl.multiple_of(step * DESTS * HIGH, DESTS * HIGH), DESTS * HIGH)
+    more = pl.ds(pl.multiple_of(NODES + step * DESTS * HIGH, DESTS * HIGH), DESTS * HIGH)
+    rank = rank_ref[rows, :]
     wanted = iota((CAP, OBS), 0).astype(F32)
-    pick = jnp.concatenate([(rank[h : h + 1, :] == wanted).astype(BF16) for h in range(HIGH)], 0)
-    out_ref[0, : HIGH * CAP, :] = jnp.dot(
-        pick, scaled_ref[...], preferred_element_type=F32
-    ).astype(BF16)
-    rhs = rhs_ref[pl.ds(pl.multiple_of(step * HIGH, HIGH), HIGH), :]
+    pick = jnp.concatenate(
+        [(rank[h : h + 1, :] == wanted).astype(BF16) for h in range(DESTS * HIGH)]
+        + [factor_ref[rows, :], factor_ref[more, :]],
+        0,
+    )
+    picked = jnp.dot(pick, scaled_ref[...], preferred_element_type=F32)
+    count = DESTS * HIGH
+    rhs = picked[count * CAP : count * CAP + count] + picked[count * CAP + count :]
+    picked = picked[: count * CAP].astype(BF16)
     top = rhs.astype(BF16).astype(F32)
-    out_ref[0, HIGH * CAP :, :] = jnp.concatenate([top, rhs - top], 0).astype(BF16)
+    rest = rhs - top
+    for d in range(DESTS):
+        out_ref[d, : HIGH * CAP, :] = picked[d * HIGH * CAP : (d + 1) * HIGH * CAP]
+        mine = slice(d * HIGH, (d + 1) * HIGH)
+        out_ref[d, HIGH * CAP :, :] = jnp.concatenate([top[mine], rest[mine]], 0).astype(BF16)
 
 
 def route(node, weight, innov, pert):
     return pl.pallas_call(
         route_kernel,
-        grid=(GROUP,),
+        grid=(GROUP // DESTS,),
         in_specs=[pl.BlockSpec(memory_space=pltpu.HBM)] * 4,
-        out_specs=pl.BlockSpec((1, ROWS, K), lambda d: (d, 0, 0)),
+        out_specs=pl.BlockSpec((DESTS, ROWS, K), lambda d: (d, 0, 0)),
         out_shape=jax.ShapeDtypeStruct((GROUP, ROWS, K), BF16),
         scratch_shapes=[
             pltpu.VMEM((NODES, OBS), F32),
             pltpu.VMEM((OBS, K), BF16),
-            pltpu.VMEM((NODES, K), F32),
+            pltpu.VMEM((2 * NODES, OBS), BF16),
             pltpu.VMEM((1, OBS), jnp.int32),
             pltpu.VMEM((1, OBS), BF16),
             pltpu.VMEM((1, OBS), BF16),
@@ -187,17 +199,22 @@
     error = gram / total
     root = None
     for step in range(NEWTON_STEPS - 1):
-        top, rest = split(error)
         half = (0.5 * error).astype(BF16)
-        dot = lambda u: jnp.dot(u, half, preferred_element_type=F32)
+
+        def times(*values):
+            parts = [p for v in values for p in split(v)]
+            out = jnp.dot(jnp.concatenate(parts, 0), half, preferred_element_type=F32)
+            return [
+                1.5 * v - (out[2 * i * K : (2 * i + 1) * K] + out[(2 * i + 1) * K : (2 * i + 2) * K])
+                for i, v in enumerate(values)
+            ]
+
         if step == 0:
             root = 1.5 * identity - half.astype(F32)
+            (error,) = times(error)
         else:
-            root_top, root_rest = split(root)
-            root = 1.5 * root - (dot(root_top) + dot(root_rest))
-        error = 1.5 * error - (dot(top) + dot(rest))
-        top, rest = split(error)
-        error = 1.5 * error - (dot(top) + dot(rest))
+            error, root = times(error, root)
+        (error,) = times(error)
     root = 1.5 * root - 0.5 * dot3(split(root), split(error))
     once = jnp.sum(root * rhs, 1, keepdims=True) / total
     mean_weight = jnp.sum(root * once, 0, keepdims=True)
@@ -271,7 +288,7 @@
 
 CX = 2
 CY = 8
-COLS = 4
+COLS = 16
 
 
 def analyse(slots, share, flips, table, state):

time: 111 us -> 109 us (0.982)
  Pallas kernels: 16.2 us -> 14.2 us
    pallas_call x1, Pallas kernels: 6.57 us -> 5.1 us  [route(): pl.pallas_call(route_kernel, grid=(GROUP // DESTS,), in_specs=[pl.BlockSp...]
where the time goes in v4:
time: 109 us
  blocking collectives  68.7 us (63%)
  starting transfers between devices  16.6 us (15%)
  Pallas kernels  14.2 us (13%)
  waiting for transfers between devices  9 us (8%)
    all_to_all x1, blocking collectives, shards(): grams = lax.all_to_all(grams, 'zh', split_axis=0, concat_axis=0, tiled=True)  42.2 us
    all_to_all x1, blocking collectives, shards(): lax.all_to_all(sent, ('x', 'zl'), split_axis=0, concat_axis=0, tiled=True)  26.6 us
    ppermute x4, starting transfers between devices, swap(): return (lax.ppermute(block, axes, even), lax.ppermute(block, axes, odd))  16.6 us
    ppermute x4, waiting for transfers between devices, swap(): return (lax.ppermute(block, axes, even), lax.ppermute(block, axes, odd))  9 us
    pallas_call x1, Pallas kernels, route(): pl.pallas_call(route_kernel, grid=(GROUP // DESTS,), in_specs=[pl.BlockSp...  5.1 us
    pallas_call x1, Pallas kernels, node_transform(): pl.pallas_call(newton_kernel, out_shape=jax.ShapeDtypeStruct((PACKED, HAL...  3.71 us
    pallas_call x1, Pallas kernels, analyse(): pl.pallas_call(analysis_kernel, grid_spec=pltpu.PrefetchScalarGridSpec(nu...  3.7 us
  transfers between devices with their start and end apart: 4, of which 2 were waited for; matrix products, arithmetic and copies ran while one was open for 0% of the time, Pallas kernels for 0%

profile of v4, /device:TPU:25, one launch (start us, length us, event | category | flops | bytes accessed | tf_op | source)
XLA Modules:
  0.0 108.9 jit_solution(309306811272888404)
XLA Ops:
  0.0 5.1 %route.1 = bf16[8,400,256]{2,1,0:T(8,128)(2,1)S(1)} custom-call(s32[1,2048]{1,0:T(1,128)} %bitcast.17, bf16[1,2048]{1,0:T(2,128)(2,1)} %weight_hbm.1, bf16[1,2048]{1,0:T(2,128)(2,1)} %innov_hbm.1, bf16[2048,256]{1,0:T(8,128)(2,1)} %bitcast.14), custom_call_target="tpu_custom_call" | custom-call | tf_op jit(solution)/shard_map/route/pallas_call | solution.py:98
  5.1 26.6 %all_to_all.10.obs_ref.side_ref = bf16[8,400,256]{2,1,0:T(8,128)(2,1)S(1)} all-to-all(bf16[8,400,256]{2,1,0:T(8,128)(2,1)S(1)} %route.1), channel_id=1, replica_groups=mesh['x'=4,'zh'=8,'zl'=2,'y'=4,'c'=2] {'x','zl'}, dimensions={0} | all-to-all | bytes 3276800 | tf_op jit(solution)/shard_map/all_to_all | solution.py:319
  31.7 1.7 %gram.1 = bf16[8,264,128]{2,1,0:T(8,128)(2,1)S(1)} custom-call(bf16[8,400,256]{2,1,0:T(8,128)(2,1)S(1)} %all_to_all.10.obs_ref.side_ref, bf16[8,400,256]{2,1,0:T(8,128)(2,1)S(1)} %all_to_all.10.obs_ref.side_ref), custom_call_target="tpu_custom_call" | custom-call | tf_op jit(solution)/shard_map/gram/pallas_call | solution.py:156
  33.4 0.0 copy-start
  33.4 0.0 copy-start.1
  33.4 0.0 copy-start.2
  33.4 42.2 %all_to_all.11.got_ref = bf16[8,264,128]{2,1,0:T(8,128)(2,1)S(1)} all-to-all(bf16[8,264,128]{2,1,0:T(8,128)(2,1)S(1)} %gram.1), channel_id=1, replica_groups=mesh['x'=4,'zh'=8,'zl'=2,'y'=4,'c'=2] {'zh'}, dimensions={0} | all-to-all | bytes 1081344 | tf_op jit(solution)/shard_map/all_to_all | solution.py:321
  75.6 3.7 %newton.1 = bf16[264,128]{1,0:T(8,128)(2,1)S(1)} custom-call(bf16[8,264,128]{2,1,0:T(8,128)(2,1)S(1)} %all_to_all.11.got_ref), custom_call_target="tpu_custom_call" | custom-call | tf_op jit(solution)/shard_map/newton/pallas_call | solution.py:234
  79.3 8.1 %collective-permute-start.1 = (bf16[264,128]{1,0:T(8,128)(2,1)S(1)}, bf16[264,128]{1,0:T(8,128)(2,1)S(1)}, u32[]{:S(2)}, u32[]{:S(2)}) collective-permute-start(bf16[264,128]{1,0:T(8,128)(2,1)S(1)} %newton.1), channel_id=1, source_target_pairs={{0,504},{8,16},{16,8},{24,32},{32,24},{40,48},{48,40},{56,64},{64,... | collective-permute-start | bytes 202760 | tf_op jit(solution)/shard_map/ppermute | solution.py:314
  87.4 2.6 %collective-permute-start = (bf16[264,128]{1,0:T(8,128)(2,1)S(1)}, bf16[264,128]{1,0:T(8,128)(2,1)S(1)}, u32[]{:S(2)}, u32[]{:S(2)}) collective-permute-start(bf16[264,128]{1,0:T(8,128)(2,1)S(1)} %newton.1), channel_id=1, source_target_pairs={{0,8},{8,0},{16,24},{24,16},{32,40},{40,32},{48,56},{56,48},{64,72... | collective-permute-start | bytes 202760 | tf_op jit(solution)/shard_map/ppermute | solution.py:314
  89.9 0.0 collective-permute-done.1
  89.9 2.8 %collective-permute-done = bf16[264,128]{1,0:T(8,128)(2,1)S(1)} collective-permute-done((bf16[264,128]{1,0:T(8,128)(2,1)S(1)}, bf16[264,128]{1,0:T(8,128)(2,1)S(1)}, u32[]{:S(2)}, u32[]{:S(2)}) %collective-permute-start) | collective-permute-done | bytes 67616 | tf_op jit(solution)/shard_map/ppermute | solution.py:314
  92.7 4.1 %collective-permute-start.2 = (bf16[3,264,128]{2,1,0:T(8,128)(2,1)S(1)}, bf16[3,264,128]{2,1,0:T(8,128)(2,1)S(1)}, u32[]{:S(2)}, u32[]{:S(2)}) collective-permute-start(bf16[3,264,128]{2,1,0:T(8,128)(2,1)S(1)} %pad_maximum_fusion), channel_id=1, source_target_pairs={{0,1},{1,0},{2,3},{3,2},{4,5},{5,4},{6,7},{7,6},{8,9},{9,8},{10,11... | collective-permute-start | bytes 608264 | tf_op jit(solution)/shard_map/ppermute | solution.py:314
  96.8 0.1 pad_add_fusion.flip_ref
  96.9 1.9 %collective-permute-start.3 = (bf16[3,264,128]{2,1,0:T(8,128)(2,1)S(1)}, bf16[3,264,128]{2,1,0:T(8,128)(2,1)S(1)}, u32[]{:S(2)}, u32[]{:S(2)}) collective-permute-start(bf16[3,264,128]{2,1,0:T(8,128)(2,1)S(1)} %pad_maximum_fusion), channel_id=1, source_target_pairs={{0,7},{1,2},{2,1},{3,4},{4,3},{5,6},{6,5},{7,0},{8,15},{9,10},{10,... | collective-permute-start | bytes 608264 | tf_op jit(solution)/shard_map/ppermute | solution.py:314
  98.8 0.0 collective-permute-done.2
  98.9 6.2 %collective-permute-done.3 = bf16[3,264,128]{2,1,0:T(8,128)(2,1)S(1)} collective-permute-done((bf16[3,264,128]{2,1,0:T(8,128)(2,1)S(1)}, bf16[3,264,128]{2,1,0:T(8,128)(2,1)S(1)}, u32[]{:S(2)}, u32[]{:S(2)}) %collective-permute-start.3) | collective-permute-done | bytes 202784 | tf_op jit(solution)/shard_map/ppermute | solution.py:314
  105.2 0.0 copy-done
  105.2 0.0 copy-done.1
  105.2 0.0 copy-done.2
  105.2 3.7 %analysis.1 = bf16[16,128,256]{2,1,0:T(8,128)(2,1)} custom-call(s32[4,2,8]{2,1,0:T(2,128)S(1)} %copy-done.1, f32[4,2,8]{2,1,0:T(2,128)S(1)} %copy-done.2, s32[2]{0:T(128)S(1)} %pad_add_fusion.flip_ref, bf16[9,264,128]{2,1,0:T(8,128)(2,1)S(1)} %constant_dynamic-update-slice_fusion.table_ref, bf16[16,128,256]{2,1,0:T(8,128)(2,1)S(1)} %bitcast.12), custom_call_target="tpu_custom_call" | custom-call | tf_op jit(solution)/shard_map/analysis/pallas_call | solution.py:297
  (6 shorter events, 0.1 us)
Async XLA Ops:
  33.4 71.8 %copy-start = (bf16[2,8,128,256]{3,2,1,0:T(8,128)(2,1)S(1)}, bf16[2,8,128,256]{3,2,1,0:T(8,128)(2,1)}, u32[]{:S(2)}) copy-start(bf16[2,8,128,256]{3,2,1,0:T(8,128)(2,1)} %param.7) | copy-start | bytes 3145732
  33.4 71.8 %copy-start.1 = (s32[4,2,8]{2,1,0:T(2,128)S(1)}, s32[4,2,8]{2,1,0:T(2,128)}, u32[]{:S(2)}) copy-start(s32[4,2,8]{2,1,0:T(2,128)} %slot_ref.1) | copy-start | bytes 772
  33.4 71.8 %copy-start.2 = (f32[4,2,8]{2,1,0:T(2,128)S(1)}, f32[4,2,8]{2,1,0:T(2,128)}, u32[]{:S(2)}) copy-start(f32[4,2,8]{2,1,0:T(2,128)} %share_ref.1) | copy-start | bytes 772
  79.3 10.6 %collective-permute-start.1 = (bf16[264,128]{1,0:T(8,128)(2,1)S(1)}, bf16[264,128]{1,0:T(8,128)(2,1)S(1)}, u32[]{:S(2)}, u32[]{:S(2)}) collective-permute-start(bf16[264,128]{1,0:T(8,128)(2,1)S(1)} %newton.1), channel_id=1, source_target_pairs={{0,504},{8,16},{16,8},{24,32},{32,24},{40,48},{48,40},{56,64},{64,... | collective-permute-start | bytes 202760 | tf_op jit(solution)/shard_map/ppermute | solution.py:314
  87.4 5.3 %collective-permute-start = (bf16[264,128]{1,0:T(8,128)(2,1)S(1)}, bf16[264,128]{1,0:T(8,128)(2,1)S(1)}, u32[]{:S(2)}, u32[]{:S(2)}) collective-permute-start(bf16[264,128]{1,0:T(8,128)(2,1)S(1)} %newton.1), channel_id=1, source_target_pairs={{0,8},{8,0},{16,24},{24,16},{32,40},{40,32},{48,56},{56,48},{64,72... | collective-permute-start | bytes 202760 | tf_op jit(solution)/shard_map/ppermute | solution.py:314
  92.7 6.1 %collective-permute-start.2 = (bf16[3,264,128]{2,1,0:T(8,128)(2,1)S(1)}, bf16[3,264,128]{2,1,0:T(8,128)(2,1)S(1)}, u32[]{:S(2)}, u32[]{:S(2)}) collective-permute-start(bf16[3,264,128]{2,1,0:T(8,128)(2,1)S(1)} %pad_maximum_fusion), channel_id=1, source_target_pairs={{0,1},{1,0},{2,3},{3,2},{4,5},{5,4},{6,7},{7,6},{8,9},{9,8},{10,11... | collective-permute-start | bytes 608264 | tf_op jit(solution)/shard_map/ppermute | solution.py:314
  96.9 8.3 %collective-permute-start.3 = (bf16[3,264,128]{2,1,0:T(8,128)(2,1)S(1)}, bf16[3,264,128]{2,1,0:T(8,128)(2,1)S(1)}, u32[]{:S(2)}, u32[]{:S(2)}) collective-permute-start(bf16[3,264,128]{2,1,0:T(8,128)(2,1)S(1)} %pad_maximum_fusion), channel_id=1, source_target_pairs={{0,7},{1,2},{2,1},{3,4},{4,3},{5,6},{6,5},{7,0},{8,15},{9,10},{10,... | collective-permute-start | bytes 608264 | tf_op jit(solution)/shard_map/ppermute | solution.py:314

commit v5 on v4

--- a/solution.py
+++ b/solution.py
@@ -5,6 +5,7 @@
 from jax.experimental.pallas import tpu as pltpu
 from jax.sharding import Mesh
 from jax.sharding import PartitionSpec as P
+
 
 NEWTON_STEPS = 8
 inflation = 1.1
@@ -239,14 +240,13 @@
     )(got)
 
 
-def analysis_kernel(slot_ref, share_ref, flip_ref, table_ref, state_ref, out_ref):
-    step = pl.program_id(0)
+def analysis_kernel(slot_ref, share_ref, flip_ref, table_ref, state_ref, out_hbm, out_ref, sems):
+    copies = []
     flip_x, flip_y = flip_ref[0], flip_ref[1]
     low, high = iota((HALF, HALF), 0), iota((HALF, HALF), 1)
     eye = low == high
     for n in range(COLS):
-        column = step * COLS + n
-        cx, cy = column // CY, column % CY
+        cx, cy = n // CY, n % CY
         shares = [share_ref[q, cx, cy] for q in range(4)]
         total = shares[0] + shares[1] + shares[2] + shares[3]
         scale = 1.0 / jnp.full((1, 1), total, F32)
@@ -284,6 +284,10 @@
             anomaly, turned, (((1,), (1,)), ((), ())), preferred_element_type=F32
         )
         out_ref[n] = (mean + update).astype(BF16)
+        copies.append(pltpu.make_async_copy(out_ref.at[n], out_hbm.at[n], sems.at[n]))
+        copies[-1].start()
+    for copy in copies:
+        copy.wait()
 
 
 CX = 2
@@ -300,7 +304,8 @@
             num_scalar_prefetch=3,
             grid=(columns // COLS,),
             in_specs=[pl.BlockSpec((9, PACKED, HALF), lambda f, *_: (0, 0, 0)), block],
-            out_specs=block,
+            out_specs=pl.BlockSpec(memory_space=pltpu.HBM),
+            scratch_shapes=[pltpu.VMEM((COLS, levels, width), BF16), pltpu.SemaphoreType.DMA((COLS,))],
         ),
         out_shape=jax.ShapeDtypeStruct(state.shape, BF16),
         name="analysis",
@@ -311,7 +316,9 @@
 def swap(block, axes, count):
     even = [(i, i ^ 1) for i in range(count)]
     odd = [(i, (((i + 1) ^ 1) - 1) % count) for i in range(count)]
-    return lax.ppermute(block, axes, even), lax.ppermute(block, axes, odd)
+    far = lax.ppermute(block, axes, odd)
+    near = lax.ppermute(block, axes, even)
+    return near, far
 
 
 def shards(members, obs_pert, obs_weight, obs_innov, obs_node, neighbour_slot, interp_weight):

time: 109 us -> 109 us (level)
  no operation moved by 1% of the time
where the time goes in v5:
time: 109 us
  blocking collectives  68.7 us (63%)
  starting transfers between devices  16.6 us (15%)
  Pallas kernels  14.1 us (13%)
  waiting for transfers between devices  9 us (8%)
    all_to_all x1, blocking collectives, shards(): grams = lax.all_to_all(grams, 'zh', split_axis=0, concat_axis=0, tiled=True)  42.2 us
    all_to_all x1, blocking collectives, shards(): lax.all_to_all(sent, ('x', 'zl'), split_axis=0, concat_axis=0, tiled=True)  26.6 us
    ppermute x2, starting transfers between devices, swap(): far = lax.ppermute(block, axes, odd)  9.97 us
    ppermute x2, starting transfers between devices, swap(): near = lax.ppermute(block, axes, even)  6.62 us
    ppermute x2, waiting for transfers between devices, swap(): far = lax.ppermute(block, axes, odd)  6.25 us
    pallas_call x1, Pallas kernels, route(): pl.pallas_call(route_kernel, grid=(GROUP // DESTS,), in_specs=[pl.BlockSp...  5.1 us
    pallas_call x1, Pallas kernels, node_transform(): pl.pallas_call(newton_kernel, out_shape=jax.ShapeDtypeStruct((PACKED, HAL...  3.71 us
    pallas_call x1, Pallas kernels, analyse(): pl.pallas_call(analysis_kernel, grid_spec=pltpu.PrefetchScalarGridSpec(nu...  3.59 us
  transfers between devices with their start and end apart: 4, of which 2 were waited for; matrix products, arithmetic and copies ran while one was open for 0% of the time, Pallas kernels for 0%

profile of v5, /device:TPU:25, one launch (start us, length us, event | category | flops | bytes accessed | tf_op | source)
XLA Modules:
  0.0 108.8 jit_solution(9985051530689623166)
XLA Ops:
  0.0 5.1 %route.1 = bf16[8,400,256]{2,1,0:T(8,128)(2,1)S(1)} custom-call(s32[1,2048]{1,0:T(1,128)} %bitcast.17, bf16[1,2048]{1,0:T(2,128)(2,1)} %weight_hbm.1, bf16[1,2048]{1,0:T(2,128)(2,1)} %innov_hbm.1, bf16[2048,256]{1,0:T(8,128)(2,1)} %bitcast.14), custom_call_target="tpu_custom_call" | custom-call | tf_op jit(solution)/shard_map/route/pallas_call | solution.py:99
  5.1 26.6 %all_to_all.10.obs_ref.side_ref = bf16[8,400,256]{2,1,0:T(8,128)(2,1)S(1)} all-to-all(bf16[8,400,256]{2,1,0:T(8,128)(2,1)S(1)} %route.1), channel_id=1, replica_groups=mesh['x'=4,'zh'=8,'zl'=2,'y'=4,'c'=2] {'x','zl'}, dimensions={0} | all-to-all | bytes 3276800 | tf_op jit(solution)/shard_map/all_to_all | solution.py:326
  31.7 1.7 %gram.1 = bf16[8,264,128]{2,1,0:T(8,128)(2,1)S(1)} custom-call(bf16[8,400,256]{2,1,0:T(8,128)(2,1)S(1)} %all_to_all.10.obs_ref.side_ref, bf16[8,400,256]{2,1,0:T(8,128)(2,1)S(1)} %all_to_all.10.obs_ref.side_ref), custom_call_target="tpu_custom_call" | custom-call | tf_op jit(solution)/shard_map/gram/pallas_call | solution.py:157
  33.4 0.0 copy-start
  33.4 0.0 copy-start.1
  33.4 0.0 copy-start.2
  33.4 42.2 %all_to_all.11.got_ref = bf16[8,264,128]{2,1,0:T(8,128)(2,1)S(1)} all-to-all(bf16[8,264,128]{2,1,0:T(8,128)(2,1)S(1)} %gram.1), channel_id=1, replica_groups=mesh['x'=4,'zh'=8,'zl'=2,'y'=4,'c'=2] {'zh'}, dimensions={0} | all-to-all | bytes 1081344 | tf_op jit(solution)/shard_map/all_to_all | solution.py:328
  75.6 3.7 %newton.1 = bf16[264,128]{1,0:T(8,128)(2,1)S(1)} custom-call(bf16[8,264,128]{2,1,0:T(8,128)(2,1)S(1)} %all_to_all.11.got_ref), custom_call_target="tpu_custom_call" | custom-call | tf_op jit(solution)/shard_map/newton/pallas_call | solution.py:235
  79.3 8.1 %collective-permute-start.1 = (bf16[264,128]{1,0:T(8,128)(2,1)S(1)}, bf16[264,128]{1,0:T(8,128)(2,1)S(1)}, u32[]{:S(2)}, u32[]{:S(2)}) collective-permute-start(bf16[264,128]{1,0:T(8,128)(2,1)S(1)} %newton.1), channel_id=1, source_target_pairs={{0,504},{8,16},{16,8},{24,32},{32,24},{40,48},{48,40},{56,64},{64,... | collective-permute-start | bytes 202760 | tf_op jit(solution)/shard_map/ppermute | solution.py:319
  87.4 2.6 %collective-permute-start = (bf16[264,128]{1,0:T(8,128)(2,1)S(1)}, bf16[264,128]{1,0:T(8,128)(2,1)S(1)}, u32[]{:S(2)}, u32[]{:S(2)}) collective-permute-start(bf16[264,128]{1,0:T(8,128)(2,1)S(1)} %newton.1), channel_id=1, source_target_pairs={{0,8},{8,0},{16,24},{24,16},{32,40},{40,32},{48,56},{56,48},{64,72... | collective-permute-start | bytes 202760 | tf_op jit(solution)/shard_map/ppermute | solution.py:320
  89.9 0.0 collective-permute-done.1
  89.9 2.8 %collective-permute-done = bf16[264,128]{1,0:T(8,128)(2,1)S(1)} collective-permute-done((bf16[264,128]{1,0:T(8,128)(2,1)S(1)}, bf16[264,128]{1,0:T(8,128)(2,1)S(1)}, u32[]{:S(2)}, u32[]{:S(2)}) %collective-permute-start) | collective-permute-done | bytes 67616 | tf_op jit(solution)/shard_map/ppermute | solution.py:320
  92.7 4.1 %collective-permute-start.2 = (bf16[3,264,128]{2,1,0:T(8,128)(2,1)S(1)}, bf16[3,264,128]{2,1,0:T(8,128)(2,1)S(1)}, u32[]{:S(2)}, u32[]{:S(2)}) collective-permute-start(bf16[3,264,128]{2,1,0:T(8,128)(2,1)S(1)} %pad_maximum_fusion), channel_id=1, source_target_pairs={{0,1},{1,0},{2,3},{3,2},{4,5},{5,4},{6,7},{7,6},{8,9},{9,8},{10,11... | collective-permute-start | bytes 608264 | tf_op jit(solution)/shard_map/ppermute | solution.py:320
  96.8 0.1 pad_add_fusion.flip_ref
  96.9 1.9 %collective-permute-start.3 = (bf16[3,264,128]{2,1,0:T(8,128)(2,1)S(1)}, bf16[3,264,128]{2,1,0:T(8,128)(2,1)S(1)}, u32[]{:S(2)}, u32[]{:S(2)}) collective-permute-start(bf16[3,264,128]{2,1,0:T(8,128)(2,1)S(1)} %pad_maximum_fusion), channel_id=1, source_target_pairs={{0,7},{1,2},{2,1},{3,4},{4,3},{5,6},{6,5},{7,0},{8,15},{9,10},{10,... | collective-permute-start | bytes 608264 | tf_op jit(solution)/shard_map/ppermute | solution.py:319
  98.8 0.0 collective-permute-done.2
  98.9 6.2 %collective-permute-done.3 = bf16[3,264,128]{2,1,0:T(8,128)(2,1)S(1)} collective-permute-done((bf16[3,264,128]{2,1,0:T(8,128)(2,1)S(1)}, bf16[3,264,128]{2,1,0:T(8,128)(2,1)S(1)}, u32[]{:S(2)}, u32[]{:S(2)}) %collective-permute-start.3) | collective-permute-done | bytes 202784 | tf_op jit(solution)/shard_map/ppermute | solution.py:319
  105.2 0.0 copy-done
  105.2 0.0 copy-done.1
  105.2 0.0 copy-done.2
  105.2 3.6 %analysis.1 = bf16[16,128,256]{2,1,0:T(8,128)(2,1)} custom-call(s32[4,2,8]{2,1,0:T(2,128)S(1)} %copy-done.1, f32[4,2,8]{2,1,0:T(2,128)S(1)} %copy-done.2, s32[2]{0:T(128)S(1)} %pad_add_fusion.flip_ref, bf16[9,264,128]{2,1,0:T(8,128)(2,1)S(1)} %constant_dynamic-update-slice_fusion.table_ref, bf16[16,128,256]{2,1,0:T(8,128)(2,1)S(1)} %bitcast.12), custom_call_target="tpu_custom_call" | custom-call | tf_op jit(solution)/shard_map/analysis/pallas_call | solution.py:301
  (6 shorter events, 0.1 us)
Async XLA Ops:
  33.4 71.8 %copy-start = (bf16[2,8,128,256]{3,2,1,0:T(8,128)(2,1)S(1)}, bf16[2,8,128,256]{3,2,1,0:T(8,128)(2,1)}, u32[]{:S(2)}) copy-start(bf16[2,8,128,256]{3,2,1,0:T(8,128)(2,1)} %param.7) | copy-start | bytes 3145732
  33.4 71.8 %copy-start.1 = (s32[4,2,8]{2,1,0:T(2,128)S(1)}, s32[4,2,8]{2,1,0:T(2,128)}, u32[]{:S(2)}) copy-start(s32[4,2,8]{2,1,0:T(2,128)} %slot_ref.1) | copy-start | bytes 772
  33.4 71.8 %copy-start.2 = (f32[4,2,8]{2,1,0:T(2,128)S(1)}, f32[4,2,8]{2,1,0:T(2,128)}, u32[]{:S(2)}) copy-start(f32[4,2,8]{2,1,0:T(2,128)} %share_ref.1) | copy-start | bytes 772
  79.3 10.6 %collective-permute-start.1 = (bf16[264,128]{1,0:T(8,128)(2,1)S(1)}, bf16[264,128]{1,0:T(8,128)(2,1)S(1)}, u32[]{:S(2)}, u32[]{:S(2)}) collective-permute-start(bf16[264,128]{1,0:T(8,128)(2,1)S(1)} %newton.1), channel_id=1, source_target_pairs={{0,504},{8,16},{16,8},{24,32},{32,24},{40,48},{48,40},{56,64},{64,... | collective-permute-start | bytes 202760 | tf_op jit(solution)/shard_map/ppermute | solution.py:319
  87.4 5.3 %collective-permute-start = (bf16[264,128]{1,0:T(8,128)(2,1)S(1)}, bf16[264,128]{1,0:T(8,128)(2,1)S(1)}, u32[]{:S(2)}, u32[]{:S(2)}) collective-permute-start(bf16[264,128]{1,0:T(8,128)(2,1)S(1)} %newton.1), channel_id=1, source_target_pairs={{0,8},{8,0},{16,24},{24,16},{32,40},{40,32},{48,56},{56,48},{64,72... | collective-permute-start | bytes 202760 | tf_op jit(solution)/shard_map/ppermute | solution.py:320
  92.7 6.1 %collective-permute-start.2 = (bf16[3,264,128]{2,1,0:T(8,128)(2,1)S(1)}, bf16[3,264,128]{2,1,0:T(8,128)(2,1)S(1)}, u32[]{:S(2)}, u32[]{:S(2)}) collective-permute-start(bf16[3,264,128]{2,1,0:T(8,128)(2,1)S(1)} %pad_maximum_fusion), channel_id=1, source_target_pairs={{0,1},{1,0},{2,3},{3,2},{4,5},{5,4},{6,7},{7,6},{8,9},{9,8},{10,11... | collective-permute-start | bytes 608264 | tf_op jit(solution)/shard_map/ppermute | solution.py:320
  96.9 8.3 %collective-permute-start.3 = (bf16[3,264,128]{2,1,0:T(8,128)(2,1)S(1)}, bf16[3,264,128]{2,1,0:T(8,128)(2,1)S(1)}, u32[]{:S(2)}, u32[]{:S(2)}) collective-permute-start(bf16[3,264,128]{2,1,0:T(8,128)(2,1)S(1)} %pad_maximum_fusion), channel_id=1, source_target_pairs={{0,7},{1,2},{2,1},{3,4},{4,3},{5,6},{6,5},{7,0},{8,15},{9,10},{10,... | collective-permute-start | bytes 608264 | tf_op jit(solution)/shard_map/ppermute | solution.py:319

commit v6 on v5

--- a/solution.py
+++ b/solution.py
@@ -8,6 +8,7 @@
 
 
 NEWTON_STEPS = 8
+COARSE_STEPS = 4
 inflation = 1.1
 
 SHAPE = (4, 8, 2, 4, 2)
@@ -25,7 +26,8 @@
 HALF = 128
 ROWS = HIGH * CAP + 16
 PACKED = K + 8
-WIRE = jnp.bfloat16
+WIRE = jnp.int16
+STEPS_16 = 32767.0
 F32 = jnp.float32
 BF16 = jnp.bfloat16
 
@@ -120,12 +122,21 @@
 PER = 2
 
 
+def code(value, bound):
+    scaled = jnp.floor(value * (STEPS_16 / bound) + 0.5)
+    return scaled.astype(jnp.int32).astype(WIRE)
+
+
+def bound_of(value):
+    most = jnp.max(jnp.max(jnp.abs(value), 1, keepdims=True), 0, keepdims=True)
+    return jnp.floor(most) + 1.0
+
+
 def gram_kernel(obs_ref, side_ref, out_ref):
     step = pl.program_id(0)
     low, high = iota((HALF, HALF), 0), iota((HALF, HALF), 1)
     eye = low == high
     keep = low <= high
-    rest = lambda v: v - v.astype(WIRE).astype(F32)
     sides = jnp.sum(side_ref[...].astype(F32), 0)
     name = iota((16, K), 0) % HIGH
     for n in range(PER):
@@ -135,22 +146,22 @@
         first_diag = jnp.sum(jnp.where(eye, first, 0.0), 0, keepdims=True)
         last_diag = jnp.sum(jnp.where(eye, last, 0.0), 0, keepdims=True)
         rhs = jnp.sum(jnp.where(name == step * PER + n, sides, 0.0), 0, keepdims=True)
-        out_ref[n, :HALF, :] = jnp.where(keep, first, last).astype(WIRE)
-        out_ref[n, HALF:K, :] = cross.astype(WIRE)
+        bound = bound_of(jnp.maximum(first_diag, last_diag))
+        rhs_bound = bound_of(rhs)
+        out_ref[n, :HALF, :] = code(jnp.where(keep, first, last), bound)
+        out_ref[n, HALF:K, :] = code(cross, bound)
         extra = jnp.concatenate(
             [
-                last_diag,
-                rest(last_diag),
-                rest(first_diag),
-                rhs[:, :HALF],
-                rhs[:, HALF:],
-                rest(rhs[:, :HALF]),
-                rest(rhs[:, HALF:]),
-                jnp.zeros((1, HALF), F32),
+                last_diag * (STEPS_16 / bound),
+                rhs[:, :HALF] * (STEPS_16 / rhs_bound),
+                rhs[:, HALF:] * (STEPS_16 / rhs_bound),
+                jnp.broadcast_to(bound, (1, HALF)),
+                jnp.broadcast_to(rhs_bound, (1, HALF)),
+                jnp.zeros((3, HALF), F32),
             ],
             0,
         )
-        out_ref[n, K:, :] = extra.astype(WIRE)
+        out_ref[n, K:, :] = jnp.floor(extra + 0.5).astype(jnp.int32).astype(WIRE)
 
 
 def partial_grams(got):
@@ -180,21 +191,25 @@
 
 
 def newton_kernel(got_ref, out_ref):
-    packed = jnp.sum(got_ref[...].astype(F32), 0)
+    packed, rhs_rows = 0.0, 0.0
+    for h in range(HIGH):
+        coded = got_ref[h].astype(jnp.int32).astype(F32)
+        packed += coded * (coded[K + 3 : K + 4] * (1.0 / STEPS_16))
+        rhs_rows += coded[K + 1 : K + 3] * (coded[K + 4 : K + 5] * (1.0 / STEPS_16))
     mixed, cross, extra = packed[:HALF], packed[HALF:K], packed[K:]
     low, high = iota((HALF, HALF), 0), iota((HALF, HALF), 1)
     eye = low == high
     base = (K - 1) / inflation
     upper = jnp.where(low < high, mixed, 0.0)
     lower = jnp.where(low > high, mixed, 0.0)
-    first_diag = jnp.where(eye, mixed + extra[2:3] + base, 0.0)
-    last_diag = jnp.where(eye, extra[0:1] + extra[1:2] + base, 0.0)
+    first_diag = jnp.where(eye, mixed + base, 0.0)
+    last_diag = jnp.where(eye, extra[0:1] + base, 0.0)
     first = upper + upper.T + first_diag
     last = lower + lower.T + last_diag
     gram = jnp.concatenate(
         [jnp.concatenate([first, cross], 1), jnp.concatenate([cross.T, last], 1)], 0
     )
-    rhs = jnp.concatenate([extra[3:4] + extra[5:6], extra[4:5] + extra[6:7]], 1)
+    rhs = jnp.concatenate([rhs_rows[0:1], rhs_rows[1:2]], 1)
     total = jnp.sum(jnp.sum(first_diag + last_diag, 1, keepdims=True), 0, keepdims=True)
     identity = (iota((K, K), 0) == iota((K, K), 1)).astype(F32)
     error = gram / total
@@ -203,6 +218,11 @@
         half = (0.5 * error).astype(BF16)
 
         def times(*values):
+            if step < COARSE_STEPS:
+                out = jnp.dot(
+                    jnp.concatenate([v.astype(BF16) for v in values], 0), half, preferred_element_type=F32
+                )
+                return [1.5 * v - out[i * K : (i + 1) * K] for i, v in enumerate(values)]
             parts = [p for v in values for p in split(v)]
             out = jnp.dot(jnp.concatenate(parts, 0), half, preferred_element_type=F32)
             return [
@@ -240,7 +260,29 @@
     )(got)
 
 
-def analysis_kernel(slot_ref, share_ref, flip_ref, table_ref, state_ref, out_hbm, out_ref, sems):
+def anomaly_kernel(state_ref, anomaly_ref, mean_ref):
+    for n in range(COLS):
+        state = state_ref[n].astype(F32)
+        mean = jnp.mean(state, -1, keepdims=True)
+        anomaly_ref[n] = (state - mean).astype(BF16)
+        mean_ref[n] = jnp.broadcast_to(mean, mean_ref.shape[1:])
+
+
+def anomalies(state):
+    columns, levels, _ = state.shape
+    return pl.pallas_call(
+        anomaly_kernel,
+        out_shape=[
+            jax.ShapeDtypeStruct(state.shape, BF16),
+            jax.ShapeDtypeStruct((columns, levels, HALF), F32),
+        ],
+        name="anomaly",
+        cost_estimate=pl.CostEstimate(flops=1 << 21, bytes_accessed=3 << 20, transcendentals=0),
+        compiler_params=pltpu.CompilerParams(vmem_limit_bytes=16 << 20),
+    )(state)
+
+
+def analysis_kernel(slot_ref, share_ref, flip_ref, table_ref, anomaly_ref, mean_ref, out_hbm, out_ref, sems):
     copies = []
     flip_x, flip_y = flip_ref[0], flip_ref[1]
     low, high = iota((HALF, HALF), 0), iota((HALF, HALF), 1)
@@ -261,29 +303,24 @@
         mixed, cross, extra = blend[:HALF], blend[HALF:K], blend[K:]
         upper = jnp.where(low <= high, mixed, 0.0)
         lower = jnp.where(low > high, mixed, jnp.where(eye, extra[0:1], 0.0))
-        first = extra[1:2] + extra[3:4]
-        last = extra[2:3] + extra[4:5]
-        plain = jnp.concatenate(
+        half = jnp.concatenate(
             [
                 jnp.concatenate([upper, cross], 1).astype(BF16),
                 jnp.concatenate([jnp.zeros_like(lower), lower], 1).astype(BF16),
             ],
             0,
         )
-        turned = jnp.concatenate(
-            [
-                jnp.concatenate([upper + first, cross + last], 1).astype(BF16),
-                jnp.concatenate([jnp.broadcast_to(first, lower.shape), lower + last], 1).astype(BF16),
-            ],
-            0,
-        )
-        state = state_ref[n].astype(F32)
-        mean = jnp.mean(state, -1, keepdims=True)
-        anomaly = (state - mean).astype(BF16)
-        update = jnp.dot(anomaly, plain, preferred_element_type=F32) + lax.dot_general(
-            anomaly, turned, (((1,), (1,)), ((), ())), preferred_element_type=F32
-        )
-        out_ref[n] = (mean + update).astype(BF16)
+        weight = jnp.concatenate([extra[1:2] + extra[3:4], extra[2:3] + extra[4:5]], 1)
+        top = weight.astype(BF16).astype(F32)
+        rows = jnp.concatenate([top, weight - top, jnp.zeros((HALF - 2, K), F32)], 0).astype(BF16)
+        anomaly = anomaly_ref[n]
+        across = (((1,), (1,)), ((), ()))
+        shift = lax.dot_general(anomaly, rows, across, preferred_element_type=F32)
+        mean = mean_ref[n] + (shift[:, 0:1] + shift[:, 1:2])
+        update = jnp.dot(anomaly, half, preferred_element_type=F32) + lax.dot_general(
+            anomaly, half, across, preferred_element_type=F32
+        )
+        out_ref[n] = (jnp.concatenate([mean, mean], 1) + update).astype(BF16)
         copies.append(pltpu.make_async_copy(out_ref.at[n], out_hbm.at[n], sems.at[n]))
         copies[-1].start()
     for copy in copies:
@@ -295,22 +332,23 @@
 COLS = 16
 
 
-def analyse(slots, share, flips, table, state):
-    columns, levels, width = state.shape
+def analyse(slots, share, flips, table, anomaly, mean):
+    columns, levels, width = anomaly.shape
     block = pl.BlockSpec((COLS, levels, width), lambda f, *_: (f, 0, 0))
+    wide = pl.BlockSpec((COLS, levels, HALF), lambda f, *_: (f, 0, 0))
     return pl.pallas_call(
         analysis_kernel,
         grid_spec=pltpu.PrefetchScalarGridSpec(
             num_scalar_prefetch=3,
             grid=(columns // COLS,),
-            in_specs=[pl.BlockSpec((9, PACKED, HALF), lambda f, *_: (0, 0, 0)), block],
+            in_specs=[pl.BlockSpec((9, PACKED, HALF), lambda f, *_: (0, 0, 0)), block, wide],
             out_specs=pl.BlockSpec(memory_space=pltpu.HBM),
             scratch_shapes=[pltpu.VMEM((COLS, levels, width), BF16), pltpu.SemaphoreType.DMA((COLS,))],
         ),
-        out_shape=jax.ShapeDtypeStruct(state.shape, BF16),
+        out_shape=jax.ShapeDtypeStruct(anomaly.shape, BF16),
         name="analysis",
         compiler_params=pltpu.CompilerParams(vmem_limit_bytes=16 << 20),
-    )(slots, share, flips, table, state)
+    )(slots, share, flips, table, anomaly, mean)
 
 
 def swap(block, axes, count):
@@ -326,14 +364,14 @@
     got = lax.all_to_all(sent, ("x", "zl"), split_axis=0, concat_axis=0, tiled=True)
     grams = partial_grams(got)
     grams = lax.all_to_all(grams, "zh", split_axis=0, concat_axis=0, tiled=True)
-    own = node_transform(grams)
+    own, members = lax.optimization_barrier((node_transform(grams), members))
+    anomaly, mean = anomalies(members.reshape(CX * CY, *members.shape[2:]))
     even, odd = swap(own, GX, 64)
     line = jnp.stack([even, own, odd])
     even, odd = swap(line, GY, 8)
     table = jnp.concatenate([even, line, odd])
     flips = jnp.stack([lax.axis_index(GX) % 2, lax.axis_index(GY) % 2]).astype(jnp.int32)
-    state = members.reshape(CX * CY, *members.shape[2:])
-    return analyse(neighbour_slot, interp_weight, flips, table, state).reshape(members.shape)
+    return analyse(neighbour_slot, interp_weight, flips, table, anomaly, mean).reshape(members.shape)
 
 
 def solution(mesh):

time: 109 us -> 109 us (level)
  no operation moved by 1% of the time
where the time goes in v6:
time: 109 us
  blocking collectives  68.7 us (63%)
  starting transfers between devices  16.7 us (15%)
  Pallas kernels  14.3 us (13%)
  waiting for transfers between devices  8.96 us (8%)
    all_to_all x1, blocking collectives, shards(): grams = lax.all_to_all(grams, 'zh', split_axis=0, concat_axis=0, tiled=True)  42.2 us
    all_to_all x1, blocking collectives, shards(): lax.all_to_all(sent, ('x', 'zl'), split_axis=0, concat_axis=0, tiled=True)  26.6 us
    ppermute x2, starting transfers between devices, swap(): far = lax.ppermute(block, axes, odd)  9.99 us
    ppermute x2, starting transfers between devices, swap(): near = lax.ppermute(block, axes, even)  6.66 us
    ppermute x2, waiting for transfers between devices, swap(): far = lax.ppermute(block, axes, odd)  6.25 us
    pallas_call x1, Pallas kernels, route(): pl.pallas_call(route_kernel, grid=(GROUP // DESTS,), in_specs=[pl.BlockSp...  5.1 us
    pallas_call x1, Pallas kernels, analyse(): pl.pallas_call(analysis_kernel, grid_spec=pltpu.PrefetchScalarGridSpec(nu...  3.32 us
    pallas_call x1, Pallas kernels, node_transform(): pl.pallas_call(newton_kernel, out_shape=jax.ShapeDtypeStruct((PACKED, HAL...  3.23 us
  transfers between devices with their start and end apart: 4, of which 2 were waited for; matrix products, arithmetic and copies ran while one was open for 0% of the time, Pallas kernels for 0%

profile of v6, /device:TPU:25, one launch (start us, length us, event | category | flops | bytes accessed | tf_op | source)
XLA Modules:
  0.0 109.0 jit_solution(3339754620080458332)
XLA Ops:
  0.0 5.1 %route.1 = bf16[8,400,256]{2,1,0:T(8,128)(2,1)S(1)} custom-call(s32[1,2048]{1,0:T(1,128)} %bitcast.17, bf16[1,2048]{1,0:T(2,128)(2,1)} %weight_hbm.1, bf16[1,2048]{1,0:T(2,128)(2,1)} %innov_hbm.1, bf16[2048,256]{1,0:T(8,128)(2,1)} %bitcast.14), custom_call_target="tpu_custom_call" | custom-call | tf_op jit(solution)/shard_map/route/pallas_call | solution.py:101
  5.1 26.6 %all_to_all.10.obs_ref.side_ref = bf16[8,400,256]{2,1,0:T(8,128)(2,1)S(1)} all-to-all(bf16[8,400,256]{2,1,0:T(8,128)(2,1)S(1)} %route.1), channel_id=1, replica_groups=mesh['x'=4,'zh'=8,'zl'=2,'y'=4,'c'=2] {'x','zl'}, dimensions={0} | all-to-all | bytes 3276800 | tf_op jit(solution)/shard_map/all_to_all | solution.py:364
  31.7 2.2 %gram.1 = s16[8,264,128]{2,1,0:T(8,128)(2,1)S(1)} custom-call(bf16[8,400,256]{2,1,0:T(8,128)(2,1)S(1)} %all_to_all.10.obs_ref.side_ref, bf16[8,400,256]{2,1,0:T(8,128)(2,1)S(1)} %all_to_all.10.obs_ref.side_ref), custom_call_target="tpu_custom_call" | custom-call | tf_op jit(solution)/shard_map/gram/pallas_call | solution.py:168
  33.9 0.0 copy-start
  33.9 42.2 %all_to_all.11.got_ref = s16[8,264,128]{2,1,0:T(8,128)(2,1)S(1)} all-to-all(s16[8,264,128]{2,1,0:T(8,128)(2,1)S(1)} %gram.1), channel_id=1, replica_groups=mesh['x'=4,'zh'=8,'zl'=2,'y'=4,'c'=2] {'zh'}, dimensions={0} | all-to-all | bytes 1081344 | tf_op jit(solution)/shard_map/all_to_all | solution.py:366
  76.1 0.0 copy-start.1
  76.1 0.0 copy-start.2
  76.1 3.2 %newton.1 = bf16[264,128]{1,0:T(8,128)(2,1)S(1)} custom-call(s16[8,264,128]{2,1,0:T(8,128)(2,1)S(1)} %all_to_all.11.got_ref), custom_call_target="tpu_custom_call" | custom-call | tf_op jit(solution)/shard_map/newton/pallas_call | solution.py:255
  79.3 8.1 %collective-permute-start.1 = (bf16[264,128]{1,0:T(8,128)(2,1)S(1)}, bf16[264,128]{1,0:T(8,128)(2,1)S(1)}, u32[]{:S(2)}, u32[]{:S(2)}) collective-permute-start(bf16[264,128]{1,0:T(8,128)(2,1)S(1)} %newton.1), channel_id=1, source_target_pairs={{0,504},{8,16},{16,8},{24,32},{32,24},{40,48},{48,40},{56,64},{64,... | collective-permute-start | bytes 202760 | tf_op jit(solution)/shard_map/ppermute | solution.py:357
  87.4 2.6 %collective-permute-start = (bf16[264,128]{1,0:T(8,128)(2,1)S(1)}, bf16[264,128]{1,0:T(8,128)(2,1)S(1)}, u32[]{:S(2)}, u32[]{:S(2)}) collective-permute-start(bf16[264,128]{1,0:T(8,128)(2,1)S(1)} %newton.1), channel_id=1, source_target_pairs={{0,8},{8,0},{16,24},{24,16},{32,40},{40,32},{48,56},{56,48},{64,72... | collective-permute-start | bytes 202760 | tf_op jit(solution)/shard_map/ppermute | solution.py:358
  90.0 0.0 collective-permute-done.1
  90.0 2.7 %collective-permute-done = bf16[264,128]{1,0:T(8,128)(2,1)S(1)} collective-permute-done((bf16[264,128]{1,0:T(8,128)(2,1)S(1)}, bf16[264,128]{1,0:T(8,128)(2,1)S(1)}, u32[]{:S(2)}, u32[]{:S(2)}) %collective-permute-start) | collective-permute-done | bytes 67616 | tf_op jit(solution)/shard_map/ppermute | solution.py:358
  92.7 4.1 %collective-permute-start.2 = (bf16[3,264,128]{2,1,0:T(8,128)(2,1)S(1)}, bf16[3,264,128]{2,1,0:T(8,128)(2,1)S(1)}, u32[]{:S(2)}, u32[]{:S(2)}) collective-permute-start(bf16[3,264,128]{2,1,0:T(8,128)(2,1)S(1)} %pad_maximum_fusion), channel_id=1, source_target_pairs={{0,1},{1,0},{2,3},{3,2},{4,5},{5,4},{6,7},{7,6},{8,9},{9,8},{10,11... | collective-permute-start | bytes 608264 | tf_op jit(solution)/shard_map/ppermute | solution.py:358
  96.8 0.1 pad_add_fusion.flip_ref
  96.9 0.0 copy-done
  96.9 0.4 anomaly.1
  97.3 1.9 %collective-permute-start.3 = (bf16[3,264,128]{2,1,0:T(8,128)(2,1)S(1)}, bf16[3,264,128]{2,1,0:T(8,128)(2,1)S(1)}, u32[]{:S(2)}, u32[]{:S(2)}) collective-permute-start(bf16[3,264,128]{2,1,0:T(8,128)(2,1)S(1)} %pad_maximum_fusion), channel_id=1, source_target_pairs={{0,7},{1,2},{2,1},{3,4},{4,3},{5,6},{6,5},{7,0},{8,15},{9,10},{10,... | collective-permute-start | bytes 608264 | tf_op jit(solution)/shard_map/ppermute | solution.py:357
  99.2 0.0 collective-permute-done.2
  99.3 6.2 %collective-permute-done.3 = bf16[3,264,128]{2,1,0:T(8,128)(2,1)S(1)} collective-permute-done((bf16[3,264,128]{2,1,0:T(8,128)(2,1)S(1)}, bf16[3,264,128]{2,1,0:T(8,128)(2,1)S(1)}, u32[]{:S(2)}, u32[]{:S(2)}) %collective-permute-start.3) | collective-permute-done | bytes 202784 | tf_op jit(solution)/shard_map/ppermute | solution.py:357
  105.6 0.0 copy-done.1
  105.6 0.0 copy-done.2
  105.6 3.3 %analysis.1 = bf16[16,128,256]{2,1,0:T(8,128)(2,1)} custom-call(s32[4,2,8]{2,1,0:T(2,128)S(1)} %copy-done.1, f32[4,2,8]{2,1,0:T(2,128)S(1)} %copy-done.2, s32[2]{0:T(128)S(1)} %pad_add_fusion.flip_ref, bf16[9,264,128]{2,1,0:T(8,128)(2,1)S(1)} %constant_dynamic-update-slice_fusion.table_ref, bf16[16,128,256]{2,1,0:T(8,128)(2,1)S(1)} %get-tuple-element.11.anomaly_ref, ...), custom_call_target="tpu_custom_call" | custom-call | tf_op jit(solution)/shard_map/analysis/pallas_call | solution.py:339
  (6 shorter events, 0.1 us)
Async XLA Ops:
  33.9 63.0 %copy-start = (bf16[2,8,128,256]{3,2,1,0:T(8,128)(2,1)S(1)}, bf16[2,8,128,256]{3,2,1,0:T(8,128)(2,1)}, u32[]{:S(2)}) copy-start(bf16[2,8,128,256]{3,2,1,0:T(8,128)(2,1)} %param.7) | copy-start | bytes 3145732
  76.1 29.5 %copy-start.1 = (s32[4,2,8]{2,1,0:T(2,128)S(1)}, s32[4,2,8]{2,1,0:T(2,128)}, u32[]{:S(2)}) copy-start(s32[4,2,8]{2,1,0:T(2,128)} %slot_ref.1) | copy-start | bytes 772
  76.1 29.5 %copy-start.2 = (f32[4,2,8]{2,1,0:T(2,128)S(1)}, f32[4,2,8]{2,1,0:T(2,128)}, u32[]{:S(2)}) copy-start(f32[4,2,8]{2,1,0:T(2,128)} %share_ref.1) | copy-start | bytes 772
  79.3 10.7 %collective-permute-start.1 = (bf16[264,128]{1,0:T(8,128)(2,1)S(1)}, bf16[264,128]{1,0:T(8,128)(2,1)S(1)}, u32[]{:S(2)}, u32[]{:S(2)}) collective-permute-start(bf16[264,128]{1,0:T(8,128)(2,1)S(1)} %newton.1), channel_id=1, source_target_pairs={{0,504},{8,16},{16,8},{24,32},{32,24},{40,48},{48,40},{56,64},{64,... | collective-permute-start | bytes 202760 | tf_op jit(solution)/shard_map/ppermute | solution.py:357
  87.4 5.3 %collective-permute-start = (bf16[264,128]{1,0:T(8,128)(2,1)S(1)}, bf16[264,128]{1,0:T(8,128)(2,1)S(1)}, u32[]{:S(2)}, u32[]{:S(2)}) collective-permute-start(bf16[264,128]{1,0:T(8,128)(2,1)S(1)} %newton.1), channel_id=1, source_target_pairs={{0,8},{8,0},{16,24},{24,16},{32,40},{40,32},{48,56},{56,48},{64,72... | collective-permute-start | bytes 202760 | tf_op jit(solution)/shard_map/ppermute | solution.py:358
  92.7 6.5 %collective-permute-start.2 = (bf16[3,264,128]{2,1,0:T(8,128)(2,1)S(1)}, bf16[3,264,128]{2,1,0:T(8,128)(2,1)S(1)}, u32[]{:S(2)}, u32[]{:S(2)}) collective-permute-start(bf16[3,264,128]{2,1,0:T(8,128)(2,1)S(1)} %pad_maximum_fusion), channel_id=1, source_target_pairs={{0,1},{1,0},{2,3},{3,2},{4,5},{5,4},{6,7},{7,6},{8,9},{9,8},{10,11... | collective-permute-start | bytes 608264 | tf_op jit(solution)/shard_map/ppermute | solution.py:358
  97.3 8.3 %collective-permute-start.3 = (bf16[3,264,128]{2,1,0:T(8,128)(2,1)S(1)}, bf16[3,264,128]{2,1,0:T(8,128)(2,1)S(1)}, u32[]{:S(2)}, u32[]{:S(2)}) collective-permute-start(bf16[3,264,128]{2,1,0:T(8,128)(2,1)S(1)} %pad_maximum_fusion), channel_id=1, source_target_pairs={{0,7},{1,2},{2,1},{3,4},{4,3},{5,6},{6,5},{7,0},{8,15},{9,10},{10,... | collective-permute-start | bytes 608264 | tf_op jit(solution)/shard_map/ppermute | solution.py:357

commit v7 on v6

--- a/solution.py
+++ b/solution.py
@@ -15,6 +15,9 @@
 AXES = ("x", "zh", "zl", "y", "c")
 GX = ("x", "zh", "zl")
 GY = ("y", "c")
+
+NEAR_ORDER = [0, 4, 2, 6, 1, 5, 3, 7]
+FAR_ORDER = [0, 4, 2, 6, 1, 5, 3, 7]
 
 NODES = 64
 HIGH = 8
@@ -52,7 +55,9 @@
             copy.start()
         copies[0].wait()
         row = iota((NODES, 1), 0)
-        name = (row // 16) * 16 + (row % 8) * 2 + (row // 8) % 2
+        entry = lambda table, at: sum(jnp.where(at == k, v, 0) for k, v in enumerate(table))
+        dest = entry(NEAR_ORDER, row // HIGH)
+        name = (dest // 2) * 16 + entry(FAR_ORDER, row % HIGH) * 2 + dest % 2
         onehot = (node_ref[...] == name).astype(F32)
         upper = (iota((K, K), 0) <= iota((K, K), 1)).astype(BF16)
         blocks = [onehot[:, b * K : (b + 1) * K] for b in range(OBS // K)]
@@ -361,9 +366,13 @@
 
 def shards(members, obs_pert, obs_weight, obs_innov, obs_node, neighbour_slot, interp_weight):
     sent = route(obs_node.reshape(1, OBS), obs_weight, obs_innov, obs_pert[0])
-    got = lax.all_to_all(sent, ("x", "zl"), split_axis=0, concat_axis=0, tiled=True)
+    got = lax.all_to_all(
+        sent, ("x", "zl"), split_axis=0, concat_axis=0, tiled=True, axis_index_groups=[NEAR_ORDER]
+    )
     grams = partial_grams(got)
-    grams = lax.all_to_all(grams, "zh", split_axis=0, concat_axis=0, tiled=True)
+    grams = lax.all_to_all(
+        grams, "zh", split_axis=0, concat_axis=0, tiled=True, axis_index_groups=[FAR_ORDER]
+    )
     own, members = lax.optimization_barrier((node_transform(grams), members))
     anomaly, mean = anomalies(members.reshape(CX * CY, *members.shape[2:]))
     even, odd = swap(own, GX, 64)

time: 109 us -> 108 us (level)
    ppermute x2, starting transfers between devices: 9.99 us -> 8.7 us  [swap(): far = lax.ppermute(block, axes, odd)]
where the time goes in v7:
time: 108 us
  blocking collectives  68.9 us (64%)
  starting transfers between devices  16 us (15%)
  Pallas kernels  14.3 us (13%)
  waiting for transfers between devices  8.44 us (8%)
    all_to_all x1, blocking collectives, shards(): lax.all_to_all(grams, 'zh', split_axis=0, concat_axis=0, tiled=True, axis...  42.5 us
    all_to_all x1, blocking collectives, shards(): lax.all_to_all(sent, ('x', 'zl'), split_axis=0, concat_axis=0, tiled=True...  26.4 us
    ppermute x2, starting transfers between devices, swap(): far = lax.ppermute(block, axes, odd)  8.7 us
    ppermute x2, starting transfers between devices, swap(): near = lax.ppermute(block, axes, even)  7.31 us
    ppermute x2, waiting for transfers between devices, swap(): far = lax.ppermute(block, axes, odd)  6.25 us
    pallas_call x1, Pallas kernels, route(): pl.pallas_call(route_kernel, grid=(GROUP // DESTS,), in_specs=[pl.BlockSp...  5.1 us
    pallas_call x1, Pallas kernels, analyse(): pl.pallas_call(analysis_kernel, grid_spec=pltpu.PrefetchScalarGridSpec(nu...  3.32 us
    pallas_call x1, Pallas kernels, node_transform(): pl.pallas_call(newton_kernel, out_shape=jax.ShapeDtypeStruct((PACKED, HAL...  3.23 us
  transfers between devices with their start and end apart: 4, of which 2 were waited for; matrix products, arithmetic and copies ran while one was open for 0% of the time, Pallas kernels for 0%

profile of v7, /device:TPU:25, one launch (start us, length us, event | category | flops | bytes accessed | tf_op | source)
XLA Modules:
  0.0 108.0 jit_solution(6280642265944577333)
XLA Ops:
  0.0 5.1 %route.1 = bf16[8,400,256]{2,1,0:T(8,128)(2,1)S(1)} custom-call(s32[1,2048]{1,0:T(1,128)} %bitcast.17, bf16[1,2048]{1,0:T(2,128)(2,1)} %weight_hbm.1, bf16[1,2048]{1,0:T(2,128)(2,1)} %innov_hbm.1, bf16[2048,256]{1,0:T(8,128)(2,1)} %bitcast.14), custom_call_target="tpu_custom_call" | custom-call | tf_op jit(solution)/shard_map/route/pallas_call | solution.py:106
  5.1 26.4 %all_to_all.10.obs_ref.side_ref = bf16[8,400,256]{2,1,0:T(8,128)(2,1)S(1)} all-to-all(bf16[8,400,256]{2,1,0:T(8,128)(2,1)S(1)} %route.1), channel_id=1, replica_groups={{0,256,128,384,8,264,136,392},{1,257,129,385,9,265,137,393},{2,258,130,..., dimensions={0} | all-to-all | bytes 3276800 | tf_op jit(solution)/shard_map/all_to_all | solution.py:369
  31.5 2.2 %gram.1 = s16[8,264,128]{2,1,0:T(8,128)(2,1)S(1)} custom-call(bf16[8,400,256]{2,1,0:T(8,128)(2,1)S(1)} %all_to_all.10.obs_ref.side_ref, bf16[8,400,256]{2,1,0:T(8,128)(2,1)S(1)} %all_to_all.10.obs_ref.side_ref), custom_call_target="tpu_custom_call" | custom-call | tf_op jit(solution)/shard_map/gram/pallas_call | solution.py:173
  33.7 0.0 copy-start
  33.7 42.5 %all_to_all.11.got_ref = s16[8,264,128]{2,1,0:T(8,128)(2,1)S(1)} all-to-all(s16[8,264,128]{2,1,0:T(8,128)(2,1)S(1)} %gram.1), channel_id=1, replica_groups={{0,64,32,96,16,80,48,112},{1,65,33,97,17,81,49,113},{2,66,34,98,18,82,5..., dimensions={0} | all-to-all | bytes 1081344 | tf_op jit(solution)/shard_map/all_to_all | solution.py:373
  76.3 0.0 copy-start.1
  76.3 0.0 copy-start.2
  76.3 3.2 %newton.1 = bf16[264,128]{1,0:T(8,128)(2,1)S(1)} custom-call(s16[8,264,128]{2,1,0:T(8,128)(2,1)S(1)} %all_to_all.11.got_ref), custom_call_target="tpu_custom_call" | custom-call | tf_op jit(solution)/shard_map/newton/pallas_call | solution.py:260
  79.5 6.8 %collective-permute-start.1 = (bf16[264,128]{1,0:T(8,128)(2,1)S(1)}, bf16[264,128]{1,0:T(8,128)(2,1)S(1)}, u32[]{:S(2)}, u32[]{:S(2)}) collective-permute-start(bf16[264,128]{1,0:T(8,128)(2,1)S(1)} %newton.1), channel_id=1, source_target_pairs={{0,504},{8,16},{16,8},{24,32},{32,24},{40,48},{48,40},{56,64},{64,... | collective-permute-start | bytes 202760 | tf_op jit(solution)/shard_map/ppermute | solution.py:362
  86.3 3.1 %collective-permute-start = (bf16[264,128]{1,0:T(8,128)(2,1)S(1)}, bf16[264,128]{1,0:T(8,128)(2,1)S(1)}, u32[]{:S(2)}, u32[]{:S(2)}) collective-permute-start(bf16[264,128]{1,0:T(8,128)(2,1)S(1)} %newton.1), channel_id=1, source_target_pairs={{0,8},{8,0},{16,24},{24,16},{32,40},{40,32},{48,56},{56,48},{64,72... | collective-permute-start | bytes 202760 | tf_op jit(solution)/shard_map/ppermute | solution.py:363
  89.4 0.0 collective-permute-done.1
  89.4 2.2 %collective-permute-done = bf16[264,128]{1,0:T(8,128)(2,1)S(1)} collective-permute-done((bf16[264,128]{1,0:T(8,128)(2,1)S(1)}, bf16[264,128]{1,0:T(8,128)(2,1)S(1)}, u32[]{:S(2)}, u32[]{:S(2)}) %collective-permute-start) | collective-permute-done | bytes 67616 | tf_op jit(solution)/shard_map/ppermute | solution.py:363
  91.6 4.2 %collective-permute-start.2 = (bf16[3,264,128]{2,1,0:T(8,128)(2,1)S(1)}, bf16[3,264,128]{2,1,0:T(8,128)(2,1)S(1)}, u32[]{:S(2)}, u32[]{:S(2)}) collective-permute-start(bf16[3,264,128]{2,1,0:T(8,128)(2,1)S(1)} %pad_maximum_fusion), channel_id=1, source_target_pairs={{0,1},{1,0},{2,3},{3,2},{4,5},{5,4},{6,7},{7,6},{8,9},{9,8},{10,11... | collective-permute-start | bytes 608264 | tf_op jit(solution)/shard_map/ppermute | solution.py:363
  95.9 0.1 pad_add_fusion.flip_ref
  95.9 0.0 copy-done
  95.9 0.4 anomaly.1
  96.3 1.9 %collective-permute-start.3 = (bf16[3,264,128]{2,1,0:T(8,128)(2,1)S(1)}, bf16[3,264,128]{2,1,0:T(8,128)(2,1)S(1)}, u32[]{:S(2)}, u32[]{:S(2)}) collective-permute-start(bf16[3,264,128]{2,1,0:T(8,128)(2,1)S(1)} %pad_maximum_fusion), channel_id=1, source_target_pairs={{0,7},{1,2},{2,1},{3,4},{4,3},{5,6},{6,5},{7,0},{8,15},{9,10},{10,... | collective-permute-start | bytes 608264 | tf_op jit(solution)/shard_map/ppermute | solution.py:362
  98.3 0.0 collective-permute-done.2
  98.4 6.2 %collective-permute-done.3 = bf16[3,264,128]{2,1,0:T(8,128)(2,1)S(1)} collective-permute-done((bf16[3,264,128]{2,1,0:T(8,128)(2,1)S(1)}, bf16[3,264,128]{2,1,0:T(8,128)(2,1)S(1)}, u32[]{:S(2)}, u32[]{:S(2)}) %collective-permute-start.3) | collective-permute-done | bytes 202784 | tf_op jit(solution)/shard_map/ppermute | solution.py:362
  104.6 0.0 copy-done.1
  104.6 0.0 copy-done.2
  104.7 3.3 %analysis.1 = bf16[16,128,256]{2,1,0:T(8,128)(2,1)} custom-call(s32[4,2,8]{2,1,0:T(2,128)S(1)} %copy-done.1, f32[4,2,8]{2,1,0:T(2,128)S(1)} %copy-done.2, s32[2]{0:T(128)S(1)} %pad_add_fusion.flip_ref, bf16[9,264,128]{2,1,0:T(8,128)(2,1)S(1)} %constant_dynamic-update-slice_fusion.table_ref, bf16[16,128,256]{2,1,0:T(8,128)(2,1)S(1)} %get-tuple-element.11.anomaly_ref, ...), custom_call_target="tpu_custom_call" | custom-call | tf_op jit(solution)/shard_map/analysis/pallas_call | solution.py:344
  (6 shorter events, 0.1 us)
Async XLA Ops:
  33.7 62.2 %copy-start = (bf16[2,8,128,256]{3,2,1,0:T(8,128)(2,1)S(1)}, bf16[2,8,128,256]{3,2,1,0:T(8,128)(2,1)}, u32[]{:S(2)}) copy-start(bf16[2,8,128,256]{3,2,1,0:T(8,128)(2,1)} %param.7) | copy-start | bytes 3145732
  76.3 28.4 %copy-start.1 = (s32[4,2,8]{2,1,0:T(2,128)S(1)}, s32[4,2,8]{2,1,0:T(2,128)}, u32[]{:S(2)}) copy-start(s32[4,2,8]{2,1,0:T(2,128)} %slot_ref.1) | copy-start | bytes 772
  76.3 28.4 %copy-start.2 = (f32[4,2,8]{2,1,0:T(2,128)S(1)}, f32[4,2,8]{2,1,0:T(2,128)}, u32[]{:S(2)}) copy-start(f32[4,2,8]{2,1,0:T(2,128)} %share_ref.1) | copy-start | bytes 772
  79.5 9.9 %collective-permute-start.1 = (bf16[264,128]{1,0:T(8,128)(2,1)S(1)}, bf16[264,128]{1,0:T(8,128)(2,1)S(1)}, u32[]{:S(2)}, u32[]{:S(2)}) collective-permute-start(bf16[264,128]{1,0:T(8,128)(2,1)S(1)} %newton.1), channel_id=1, source_target_pairs={{0,504},{8,16},{16,8},{24,32},{32,24},{40,48},{48,40},{56,64},{64,... | collective-permute-start | bytes 202760 | tf_op jit(solution)/shard_map/ppermute | solution.py:362
  86.3 5.3 %collective-permute-start = (bf16[264,128]{1,0:T(8,128)(2,1)S(1)}, bf16[264,128]{1,0:T(8,128)(2,1)S(1)}, u32[]{:S(2)}, u32[]{:S(2)}) collective-permute-start(bf16[264,128]{1,0:T(8,128)(2,1)S(1)} %newton.1), channel_id=1, source_target_pairs={{0,8},{8,0},{16,24},{24,16},{32,40},{40,32},{48,56},{56,48},{64,72... | collective-permute-start | bytes 202760 | tf_op jit(solution)/shard_map/ppermute | solution.py:363
  91.6 6.6 %collective-permute-start.2 = (bf16[3,264,128]{2,1,0:T(8,128)(2,1)S(1)}, bf16[3,264,128]{2,1,0:T(8,128)(2,1)S(1)}, u32[]{:S(2)}, u32[]{:S(2)}) collective-permute-start(bf16[3,264,128]{2,1,0:T(8,128)(2,1)S(1)} %pad_maximum_fusion), channel_id=1, source_target_pairs={{0,1},{1,0},{2,3},{3,2},{4,5},{5,4},{6,7},{7,6},{8,9},{9,8},{10,11... | collective-permute-start | bytes 608264 | tf_op jit(solution)/shard_map/ppermute | solution.py:363
  96.3 8.3 %collective-permute-start.3 = (bf16[3,264,128]{2,1,0:T(8,128)(2,1)S(1)}, bf16[3,264,128]{2,1,0:T(8,128)(2,1)S(1)}, u32[]{:S(2)}, u32[]{:S(2)}) collective-permute-start(bf16[3,264,128]{2,1,0:T(8,128)(2,1)S(1)} %pad_maximum_fusion), channel_id=1, source_target_pairs={{0,7},{1,2},{2,1},{3,4},{4,3},{5,6},{6,5},{7,0},{8,15},{9,10},{10,... | collective-permute-start | bytes 608264 | tf_op jit(solution)/shard_map/ppermute | solution.py:362

commit v8 on v7

--- a/solution.py
+++ b/solution.py
@@ -124,12 +124,11 @@
     )(*[pltpu.with_memory_space_constraint(v, pltpu.HBM) for v in (node, weight, innov, pert)])
 
 
-PER = 2
+PER = 4
 
 
 def code(value, bound):
-    scaled = jnp.floor(value * (STEPS_16 / bound) + 0.5)
-    return scaled.astype(jnp.int32).astype(WIRE)
+    return jnp.round(value * (STEPS_16 / bound)).astype(jnp.int32).astype(WIRE)
 
 
 def bound_of(value):

time: 108 us -> 107 us (level)
  no operation moved by 1% of the time
where the time goes in v8:
time: 107 us
  blocking collectives  68.9 us (64%)
  starting transfers between devices  16 us (15%)
  Pallas kernels  13.5 us (13%)
  waiting for transfers between devices  8.45 us (8%)
    all_to_all x1, blocking collectives, shards(): lax.all_to_all(grams, 'zh', split_axis=0, concat_axis=0, tiled=True, axis...  42.5 us
    all_to_all x1, blocking collectives, shards(): lax.all_to_all(sent, ('x', 'zl'), split_axis=0, concat_axis=0, tiled=True...  26.4 us
    ppermute x2, starting transfers between devices, swap(): far = lax.ppermute(block, axes, odd)  8.71 us
    ppermute x2, starting transfers between devices, swap(): near = lax.ppermute(block, axes, even)  7.29 us
    ppermute x2, waiting for transfers between devices, swap(): far = lax.ppermute(block, axes, odd)  6.25 us
    pallas_call x1, Pallas kernels, route(): pl.pallas_call(route_kernel, grid=(GROUP // DESTS,), in_specs=[pl.BlockSp...  5.1 us
    pallas_call x1, Pallas kernels, analyse(): pl.pallas_call(analysis_kernel, grid_spec=pltpu.PrefetchScalarGridSpec(nu...  3.32 us
    pallas_call x1, Pallas kernels, node_transform(): pl.pallas_call(newton_kernel, out_shape=jax.ShapeDtypeStruct((PACKED, HAL...  3.22 us
  transfers between devices with their start and end apart: 4, of which 2 were waited for; matrix products, arithmetic and copies ran while one was open for 0% of the time, Pallas kernels for 0%

profile of v8, /device:TPU:25, one launch (start us, length us, event | category | flops | bytes accessed | tf_op | source)
XLA Modules:
  0.0 107.2 jit_solution(5599040012830686310)
XLA Ops:
  0.0 5.1 %route.1 = bf16[8,400,256]{2,1,0:T(8,128)(2,1)S(1)} custom-call(s32[1,2048]{1,0:T(1,128)} %bitcast.17, bf16[1,2048]{1,0:T(2,128)(2,1)} %weight_hbm.1, bf16[1,2048]{1,0:T(2,128)(2,1)} %innov_hbm.1, bf16[2048,256]{1,0:T(8,128)(2,1)} %bitcast.14), custom_call_target="tpu_custom_call" | custom-call | tf_op jit(solution)/shard_map/route/pallas_call | solution.py:106
  5.1 26.4 %all_to_all.10.obs_ref.side_ref = bf16[8,400,256]{2,1,0:T(8,128)(2,1)S(1)} all-to-all(bf16[8,400,256]{2,1,0:T(8,128)(2,1)S(1)} %route.1), channel_id=1, replica_groups={{0,256,128,384,8,264,136,392},{1,257,129,385,9,265,137,393},{2,258,130,..., dimensions={0} | all-to-all | bytes 3276800 | tf_op jit(solution)/shard_map/all_to_all | solution.py:368
  31.5 1.4 %gram.1 = s16[8,264,128]{2,1,0:T(8,128)(2,1)S(1)} custom-call(bf16[8,400,256]{2,1,0:T(8,128)(2,1)S(1)} %all_to_all.10.obs_ref.side_ref, bf16[8,400,256]{2,1,0:T(8,128)(2,1)S(1)} %all_to_all.10.obs_ref.side_ref), custom_call_target="tpu_custom_call" | custom-call | tf_op jit(solution)/shard_map/gram/pallas_call | solution.py:172
  32.9 0.0 copy-start
  32.9 42.5 %all_to_all.11.got_ref = s16[8,264,128]{2,1,0:T(8,128)(2,1)S(1)} all-to-all(s16[8,264,128]{2,1,0:T(8,128)(2,1)S(1)} %gram.1), channel_id=1, replica_groups={{0,64,32,96,16,80,48,112},{1,65,33,97,17,81,49,113},{2,66,34,98,18,82,5..., dimensions={0} | all-to-all | bytes 1081344 | tf_op jit(solution)/shard_map/all_to_all | solution.py:372
  75.5 0.0 copy-start.1
  75.5 0.0 copy-start.2
  75.5 3.2 %newton.1 = bf16[264,128]{1,0:T(8,128)(2,1)S(1)} custom-call(s16[8,264,128]{2,1,0:T(8,128)(2,1)S(1)} %all_to_all.11.got_ref), custom_call_target="tpu_custom_call" | custom-call | tf_op jit(solution)/shard_map/newton/pallas_call | solution.py:259
  78.7 6.8 %collective-permute-start.1 = (bf16[264,128]{1,0:T(8,128)(2,1)S(1)}, bf16[264,128]{1,0:T(8,128)(2,1)S(1)}, u32[]{:S(2)}, u32[]{:S(2)}) collective-permute-start(bf16[264,128]{1,0:T(8,128)(2,1)S(1)} %newton.1), channel_id=1, source_target_pairs={{0,504},{8,16},{16,8},{24,32},{32,24},{40,48},{48,40},{56,64},{64,... | collective-permute-start | bytes 202760 | tf_op jit(solution)/shard_map/ppermute | solution.py:361
  85.5 3.1 %collective-permute-start = (bf16[264,128]{1,0:T(8,128)(2,1)S(1)}, bf16[264,128]{1,0:T(8,128)(2,1)S(1)}, u32[]{:S(2)}, u32[]{:S(2)}) collective-permute-start(bf16[264,128]{1,0:T(8,128)(2,1)S(1)} %newton.1), channel_id=1, source_target_pairs={{0,8},{8,0},{16,24},{24,16},{32,40},{40,32},{48,56},{56,48},{64,72... | collective-permute-start | bytes 202760 | tf_op jit(solution)/shard_map/ppermute | solution.py:362
  88.6 0.0 collective-permute-done.1
  88.6 2.2 %collective-permute-done = bf16[264,128]{1,0:T(8,128)(2,1)S(1)} collective-permute-done((bf16[264,128]{1,0:T(8,128)(2,1)S(1)}, bf16[264,128]{1,0:T(8,128)(2,1)S(1)}, u32[]{:S(2)}, u32[]{:S(2)}) %collective-permute-start) | collective-permute-done | bytes 67616 | tf_op jit(solution)/shard_map/ppermute | solution.py:362
  90.8 4.2 %collective-permute-start.2 = (bf16[3,264,128]{2,1,0:T(8,128)(2,1)S(1)}, bf16[3,264,128]{2,1,0:T(8,128)(2,1)S(1)}, u32[]{:S(2)}, u32[]{:S(2)}) collective-permute-start(bf16[3,264,128]{2,1,0:T(8,128)(2,1)S(1)} %pad_maximum_fusion), channel_id=1, source_target_pairs={{0,1},{1,0},{2,3},{3,2},{4,5},{5,4},{6,7},{7,6},{8,9},{9,8},{10,11... | collective-permute-start | bytes 608264 | tf_op jit(solution)/shard_map/ppermute | solution.py:362
  95.1 0.1 pad_add_fusion.flip_ref
  95.1 0.0 copy-done
  95.1 0.4 anomaly.1
  95.5 1.9 %collective-permute-start.3 = (bf16[3,264,128]{2,1,0:T(8,128)(2,1)S(1)}, bf16[3,264,128]{2,1,0:T(8,128)(2,1)S(1)}, u32[]{:S(2)}, u32[]{:S(2)}) collective-permute-start(bf16[3,264,128]{2,1,0:T(8,128)(2,1)S(1)} %pad_maximum_fusion), channel_id=1, source_target_pairs={{0,7},{1,2},{2,1},{3,4},{4,3},{5,6},{6,5},{7,0},{8,15},{9,10},{10,... | collective-permute-start | bytes 608264 | tf_op jit(solution)/shard_map/ppermute | solution.py:361
  97.5 0.0 collective-permute-done.2
  97.6 6.2 %collective-permute-done.3 = bf16[3,264,128]{2,1,0:T(8,128)(2,1)S(1)} collective-permute-done((bf16[3,264,128]{2,1,0:T(8,128)(2,1)S(1)}, bf16[3,264,128]{2,1,0:T(8,128)(2,1)S(1)}, u32[]{:S(2)}, u32[]{:S(2)}) %collective-permute-start.3) | collective-permute-done | bytes 202784 | tf_op jit(solution)/shard_map/ppermute | solution.py:361
  103.8 0.0 copy-done.1
  103.8 0.0 copy-done.2
  103.9 3.3 %analysis.1 = bf16[16,128,256]{2,1,0:T(8,128)(2,1)} custom-call(s32[4,2,8]{2,1,0:T(2,128)S(1)} %copy-done.1, f32[4,2,8]{2,1,0:T(2,128)S(1)} %copy-done.2, s32[2]{0:T(128)S(1)} %pad_add_fusion.flip_ref, bf16[9,264,128]{2,1,0:T(8,128)(2,1)S(1)} %constant_dynamic-update-slice_fusion.table_ref, bf16[16,128,256]{2,1,0:T(8,128)(2,1)S(1)} %get-tuple-element.11.anomaly_ref, ...), custom_call_target="tpu_custom_call" | custom-call | tf_op jit(solution)/shard_map/analysis/pallas_call | solution.py:343
  (6 shorter events, 0.1 us)
Async XLA Ops:
  32.9 62.2 %copy-start = (bf16[2,8,128,256]{3,2,1,0:T(8,128)(2,1)S(1)}, bf16[2,8,128,256]{3,2,1,0:T(8,128)(2,1)}, u32[]{:S(2)}) copy-start(bf16[2,8,128,256]{3,2,1,0:T(8,128)(2,1)} %param.7) | copy-start | bytes 3145732
  75.5 28.4 %copy-start.1 = (s32[4,2,8]{2,1,0:T(2,128)S(1)}, s32[4,2,8]{2,1,0:T(2,128)}, u32[]{:S(2)}) copy-start(s32[4,2,8]{2,1,0:T(2,128)} %slot_ref.1) | copy-start | bytes 772
  75.5 28.4 %copy-start.2 = (f32[4,2,8]{2,1,0:T(2,128)S(1)}, f32[4,2,8]{2,1,0:T(2,128)}, u32[]{:S(2)}) copy-start(f32[4,2,8]{2,1,0:T(2,128)} %share_ref.1) | copy-start | bytes 772
  78.7 9.9 %collective-permute-start.1 = (bf16[264,128]{1,0:T(8,128)(2,1)S(1)}, bf16[264,128]{1,0:T(8,128)(2,1)S(1)}, u32[]{:S(2)}, u32[]{:S(2)}) collective-permute-start(bf16[264,128]{1,0:T(8,128)(2,1)S(1)} %newton.1), channel_id=1, source_target_pairs={{0,504},{8,16},{16,8},{24,32},{32,24},{40,48},{48,40},{56,64},{64,... | collective-permute-start | bytes 202760 | tf_op jit(solution)/shard_map/ppermute | solution.py:361
  85.5 5.3 %collective-permute-start = (bf16[264,128]{1,0:T(8,128)(2,1)S(1)}, bf16[264,128]{1,0:T(8,128)(2,1)S(1)}, u32[]{:S(2)}, u32[]{:S(2)}) collective-permute-start(bf16[264,128]{1,0:T(8,128)(2,1)S(1)} %newton.1), channel_id=1, source_target_pairs={{0,8},{8,0},{16,24},{24,16},{32,40},{40,32},{48,56},{56,48},{64,72... | collective-permute-start | bytes 202760 | tf_op jit(solution)/shard_map/ppermute | solution.py:362
  90.8 6.6 %collective-permute-start.2 = (bf16[3,264,128]{2,1,0:T(8,128)(2,1)S(1)}, bf16[3,264,128]{2,1,0:T(8,128)(2,1)S(1)}, u32[]{:S(2)}, u32[]{:S(2)}) collective-permute-start(bf16[3,264,128]{2,1,0:T(8,128)(2,1)S(1)} %pad_maximum_fusion), channel_id=1, source_target_pairs={{0,1},{1,0},{2,3},{3,2},{4,5},{5,4},{6,7},{7,6},{8,9},{9,8},{10,11... | collective-permute-start | bytes 608264 | tf_op jit(solution)/shard_map/ppermute | solution.py:362
  95.5 8.3 %collective-permute-start.3 = (bf16[3,264,128]{2,1,0:T(8,128)(2,1)S(1)}, bf16[3,264,128]{2,1,0:T(8,128)(2,1)S(1)}, u32[]{:S(2)}, u32[]{:S(2)}) collective-permute-start(bf16[3,264,128]{2,1,0:T(8,128)(2,1)S(1)} %pad_maximum_fusion), channel_id=1, source_target_pairs={{0,7},{1,2},{2,1},{3,4},{4,3},{5,6},{6,5},{7,0},{8,15},{9,10},{10,... | collective-permute-start | bytes 608264 | tf_op jit(solution)/shard_map/ppermute | solution.py:361
